TPU v7x, 32 devices: a whole 2x2x4 slice. The times are simulated.
32 devices in a mesh: head: 8 (over z, y), dp: 4 (over x, core).
Axes of the slice: x: 2, y: 2, z: 4, core: 2. Of those that a mesh axis runs over, the one named last changes fastest.
Arguments:
- attn_out: bfloat16 [1024, 8192], P('dp', 'head'), may hold values from -6 to 6
- head_mask: int32 [64], P('head'), may hold values from 0 to 1, as said below
- gate_scale: float32 [64], P('head'), may hold values from 0.25 to 2
- w_out: bfloat16 [8192, 8192], P('head', 'dp'), may hold values from -0.09375 to 0.09375
- grad_out: bfloat16 [1024, 8192], P(('dp', 'head')), may hold values from -6 to 6
Outputs:
- proj_out: bfloat16 [1024, 8192], P(('dp', 'head'))
- grad_attn: bfloat16 [1024, 8192], P('dp', 'head')
- grad_w: float32 [8192, 8192], P('head', 'dp')
Inputs may be any that keep to these rules, and one draw needn't show every extreme that they name: `head_mask`: exactly 32 heads are live.
All inputs are finite; a program needn't handle non-finite values.
Results may differ from a plain program's by a relative error of at most 0.0051.
Values may be sent and summed in bfloat16 or wider, within the bound.
A program may use at most 128 MiB of HBM per device.

v0:
```python
import functools

import jax
import jax.numpy as jnp
from jax import lax
from jax.experimental import pallas as pl
from jax.experimental.pallas import tpu as pltpu
from jax.sharding import PartitionSpec as P

MESH = pl.DeviceIdType.MESH
F32, BF16 = jnp.float32, jnp.bfloat16
TILE = 256
LEAD, EVERY = 3, 3
N1, N2, N3 = 2, 1, 2
VMEM_LIMIT = 62 * 1024 * 1024


def kernel(nh, nd, attn, gate, grad, w_hbm, proj, gattn, gw_hbm,
           blocks, gated, w, g, ps, po, ry, sz, rz, fin, pj, bs, bo, br, bs2, br2, stage,
           ssem, rsem, lsem, osem):
    na, nx = nh // 2, nd // 2
    h, d = lax.axis_index("head"), lax.axis_index("dp")
    a, b = h // 2, h % 2
    x, c = d // 2, d % 2
    rows, cols = fin.shape[1:]
    width = attn.shape[1]
    other = a * 2 + 1 - b
    sibling = x * 2 + 1 - c
    copies = []

    def send(src, dst, hh, dd):
        i = len(copies)
        copy = pltpu.make_async_remote_copy(
            src_ref=src, dst_ref=dst, send_sem=ssem.at[i], recv_sem=rsem.at[i],
            device_id={"head": hh, "dp": dd}, device_id_type=MESH,
        )
        copy.start()
        copies.append(copy)
        return copy

    shifts = [(kx, kc) for kx in range(nx) for kc in range(2)]
    apart = [s for s in shifts if s[0]] + [(0, 1)]
    near = [(0, 1)] + [s for s in shifts if s[0]]

    def ahead(s):
        return ((x + s[0]) % nx) * 2 + (c + s[1]) % 2

    def behind(s):
        return (x + nx - s[0]) % nx, (c + s[1]) % 2

    w_copy = pltpu.make_async_copy(w_hbm, w, lsem)
    w_copy.start()
    barrier = pltpu.get_barrier_semaphore()
    for s in near:
        pl.semaphore_signal(barrier, inc=1, device_id={"head": h, "dp": ahead(s)}, device_id_type=MESH)
    for k in range(1, nh):
        pl.semaphore_signal(barrier, inc=1, device_id={"head": (h + k) % nh, "dp": d}, device_id_type=MESH)
    pl.semaphore_wait(barrier, nd + nh - 2)

    def part(q):
        return grad.at[:, pl.ds(pl.multiple_of(q * cols, 128), cols)]

    swap = {}
    for s in apart:
        swap[s] = send(part(ahead(s)), g.at[b, x, c, a], h, ahead(s))
    across, up = {}, {}

    def spread(src, s):
        qx, qc = behind(s)
        up[s, 0] = send(src, g.at[b, qx, qc, a], other, d)
        for k in range(1, na):
            across[s, k] = send(src, g.at[b, qx, qc, a], ((a + k) % na) * 2 + b, d)

    spread(part(d), (0, 0))
    attn_x = {k: send(attn, blocks.at[x, c], h, ((x + k) % nx) * 2 + c) for k in range(1, nx)}
    attn_c = send(attn, blocks.at[x, c], h, sibling)
    g[b, x, c, a] = grad[:, pl.ds(pl.multiple_of(d * cols, 128), cols)]
    for s in near:
        swap[s].wait_recv()
        qx, qc = behind(s)
        spread(g.at[b, qx, qc, a], s)

    def forward(s, k):
        across[s, k].wait_recv()
        qx, qc = behind(s)
        ref = g.at[b, qx, qc, (a + na - k) % na]
        up[s, k] = send(ref, ref, other, d)

    for k in range(1, na):
        forward((0, 0), k)

    def put(val, qx, qc):
        val = (val.astype(F32) * gate[...]).astype(BF16).reshape(na, 2, rows, width)
        for bb in range(2):
            gated[bb, qx, qc] = val[:, bb]

    put(attn[...], x, c)
    attn_c.wait_recv()
    put(blocks[x, 1 - c], x, 1 - c)
    passed = {}
    for k in range(1, nx):
        attn_x[k].wait_recv()
        qx = (x + nx - k) % nx
        passed[k] = send(blocks.at[qx, c], blocks.at[qx, c], h, sibling)
        put(blocks[qx, c], qx, c)
    for k in range(1, nx):
        passed[k].wait_recv()
        qx = (x + nx - k) % nx
        put(blocks[qx, 1 - c], qx, 1 - c)
    w_copy.wait()

    def project(bb, out):
        @pl.loop(0, cols // TILE)
        def _(t):
            at = pl.ds(pl.multiple_of(t * TILE, TILE), TILE)
            lhs = gated[bb].reshape(nd * na * rows, width)
            res = jnp.dot(lhs, w[:, at], preferred_element_type=F32)
            out[:, :, :, at] = res.astype(out.dtype).reshape(nd, na, rows, TILE)

    project(1 - b, ps)

    to_y, to_z = {}, {}
    owners = apart + [(0, 0)]
    order = [(s, k) for s in owners for k in list(range(1, na)) + [0]]

    def send_y(s, k):
        q, to = ahead(s), (a + k) % na
        to_y[s, k] = send(ps.at[q, to], ry.at[q, to], other, d)

    def send_z(s, k):
        q, to = ahead(s), (a + k) % na
        to_y[s, k].wait_recv()
        if k:
            sz[q, to] = (po[q, to] + ry[q, to].astype(F32)).astype(BF16)
            to_z[s, k] = send(sz.at[q, to], rz.at[k - 1, q], to * 2 + b, d)

    later = [(s, k) for s in near for k in range(1, na)]
    ready, sent = list(order), []
    for _ in range(LEAD):
        sent.append(ready.pop(0))
        send_y(*sent[-1])
    project(b, po)
    for n, (s, k) in enumerate(later):
        forward(s, k)
        if EVERY and n % EVERY == EVERY - 1:
            sent.append(ready.pop(0))
            send_y(*sent[-1])
    for s, k in ready:
        send_y(s, k)
    sent += ready

    def drain(n):
        for _ in range(min(n, len(sent))):
            send_z(*sent.pop(0))

    drain(LEAD)
    for k in range(na):
        for s in shifts:
            up[s, k].wait_recv()

    def back(cc, out):
        @pl.loop(0, width // TILE)
        def _(t):
            at = pl.ds(pl.multiple_of(t * TILE, TILE), TILE)
            lhs = g[:, :, cc].reshape(2 * nx * na * rows, cols)
            res = lax.dot_general(lhs, w[at, :], (((1,), (1,)), ((), ())), preferred_element_type=F32)
            out[:, :, :, :, at] = res.astype(out.dtype).reshape(2, nx, na, rows, TILE)

    back(1 - c, bs)
    pair = send(bs, br, h, sibling)
    drain(N1)
    back(c, bo)
    drain(N2)
    pair.wait_recv()
    to_x = {}
    for k in range(1, nx):
        to = (x + k) % nx
        bs2[k - 1] = (bo[:, to] + br[:, to].astype(F32)).astype(BF16)
        to_x[k] = send(bs2.at[k - 1], br2.at[k - 1], h, to * 2 + c)

    home = {}

    def finish(s):
        q = ahead(s)
        total = po[q, a] + ry[q, a].astype(F32)
        for k in range(1, na):
            to_z[s, k].wait_recv()
            total += rz[k - 1, q].astype(F32)
        if s == (0, 0):
            pj[d] = total.astype(BF16)
        else:
            fin[q] = total.astype(BF16)
            home[s] = send(fin.at[q], pj.at[d], h, q)

    def out_copy(t, slot):
        return pltpu.make_async_copy(
            stage.at[slot], gw_hbm.at[pl.ds(pl.multiple_of(t * TILE, TILE), TILE), :], osem.at[slot])

    tiles = width // TILE

    def weight_tile(t):
        slot = t % 2
        if t >= 2:
            out_copy(t - 2, slot).wait()
        at = pl.ds(t * TILE, TILE)
        lhs = gated[:, :, :, :, :, at].reshape(nd * nh * rows, TILE).T

        @pl.loop(0, cols // (2 * TILE))
        def _(n):
            to = pl.ds(pl.multiple_of(n * 2 * TILE, 2 * TILE), 2 * TILE)
            rhs = g[:, :, :, :, :, to].reshape(nd * nh * rows, 2 * TILE)
            stage[slot, :, to] = jnp.dot(lhs, rhs, preferred_element_type=F32)

        out_copy(t, slot).start()

    for t in range(tiles):
        drain(N3)
        weight_tile(t)
    drain(len(sent))
    for s in owners:
        finish(s)

    for k in range(1, nx):
        to_x[k].wait_recv()
    total = bo[:, x] + br[:, x].astype(F32)
    for k in range(1, nx):
        total += br2[k - 1].astype(F32)
    total = (total * gate[...].reshape(1, 1, 1, width)).astype(BF16)
    for bb in range(2):
        gattn[:, bb] = total[bb]

    for s in apart:
        home[s].wait_recv()
    for q in range(nd):
        proj[:, q * cols:(q + 1) * cols] = pj[q]
    for t in range(max(tiles - 2, 0), tiles):
        out_copy(t, t % 2).wait()
    for copy in copies:
        copy.wait_send()


def fused(nh, nd, attn_out, col_gate, w_out, grad_out):
    na, nx = nh // 2, nd // 2
    rows, cols, width = grad_out.shape[0], w_out.shape[1], w_out.shape[0]
    n_sems = 2 * nd + nx * 4 + nd * nh + nd * nh + nd * na * 2
    vmem = pl.BlockSpec(memory_space=pltpu.VMEM)
    hbm = pl.BlockSpec(memory_space=pl.ANY)
    proj, gattn, gw = pl.pallas_call(
        functools.partial(kernel, nh, nd),
        out_shape=(
            jax.ShapeDtypeStruct(grad_out.shape, BF16),
            jax.ShapeDtypeStruct((na, 2, rows, width), BF16),
            jax.ShapeDtypeStruct(w_out.shape, F32),
        ),
        in_specs=[vmem, vmem, vmem, hbm],
        out_specs=(vmem, vmem, hbm),
        scratch_shapes=[
            pltpu.VMEM((nx, 2, nh * rows, width), BF16),
            pltpu.VMEM((2, nx, 2, na, rows, width), BF16),
            pltpu.VMEM(w_out.shape, BF16),
            pltpu.VMEM((2, nx, 2, na, rows, cols), BF16),
            pltpu.VMEM((nd, na, rows, cols), BF16),
            pltpu.VMEM((nd, na, rows, cols), F32),
            pltpu.VMEM((nd, na, rows, cols), BF16),
            pltpu.VMEM((nd, na, rows, cols), BF16),
            pltpu.VMEM((na - 1, nd, rows, cols), BF16),
            pltpu.VMEM((nd, rows, cols), BF16),
            pltpu.VMEM((nd, rows, cols), BF16),
            pltpu.VMEM((2, nx, na, rows, width), BF16),
            pltpu.VMEM((2, nx, na, rows, width), F32),
            pltpu.VMEM((2, nx, na, rows, width), BF16),
            pltpu.VMEM((nx - 1, 2, na, rows, width), BF16),
            pltpu.VMEM((nx - 1, 2, na, rows, width), BF16),
            pltpu.VMEM((2, TILE, cols), F32),
            pltpu.SemaphoreType.DMA((n_sems,)),
            pltpu.SemaphoreType.DMA((n_sems,)),
            pltpu.SemaphoreType.DMA,
            pltpu.SemaphoreType.DMA((2,)),
        ],
        compiler_params=pltpu.CompilerParams(
            collective_id=0, has_side_effects=True, vmem_limit_bytes=VMEM_LIMIT
        ),
    )(attn_out, col_gate.reshape(1, width), grad_out, w_out)
    return proj, gattn.reshape(attn_out.shape), gw


def shards(attn_out, head_mask, gate_scale, w_out, grad_out):
    n_dp, n_head = lax.axis_size("dp"), lax.axis_size("head")
    gate_vals = head_mask.astype(jnp.float32) * gate_scale
    width_each = attn_out.shape[1] // gate_vals.shape[0]
    col_gate = jnp.repeat(gate_vals, width_each)
    rows, (width, cols) = grad_out.shape[0], w_out.shape
    if rows % 16 == 0 and n_dp % 2 == 0 and n_head % 2 == 0 and min(n_dp, n_head) > 2 and width % TILE == 0 and cols % (2 * TILE) == 0:
        return fused(n_head, n_dp, attn_out, col_gate, w_out, grad_out)
    gated = (attn_out.astype(jnp.float32) * col_gate[None, :]).astype(jnp.bfloat16)
    mine = lax.all_to_all(grad_out, "dp", 1, 0, tiled=True)
    every = lax.all_gather(mine.reshape(n_dp, rows, cols), "head", axis=1)
    grad_cols = every.reshape(n_dp * n_head * rows, cols)
    gated_all = lax.all_gather(gated, "dp", axis=0, tiled=True)
    part = jnp.dot(gated_all, w_out, preferred_element_type=jnp.float32).astype(jnp.bfloat16)
    summed = lax.psum_scatter(part.reshape(n_dp, n_head, rows, cols), "head", scatter_dimension=1, tiled=False)
    proj_out = lax.all_to_all(summed.reshape(n_dp * rows, cols), "dp", 0, 1, tiled=True)
    back = lax.dot_general(grad_cols, w_out, (((1,), (1,)), ((), ())), preferred_element_type=jnp.float32)
    back = lax.psum_scatter(back.astype(jnp.bfloat16), "dp", scatter_dimension=0, tiled=True)
    grad_attn = (back.astype(jnp.float32) * col_gate[None, :]).astype(jnp.bfloat16)
    grad_w = lax.dot_general(gated_all, grad_cols, (((0,), (0,)), ((), ())), preferred_element_type=jnp.float32)
    return (proj_out, grad_attn, grad_w)


def solution(mesh):
    return jax.shard_map(
        shards,
        mesh=mesh,
        in_specs=(P("dp", "head"), P("head"), P("head"), P("head", "dp"), P(("dp", "head"), None)),
        out_specs=(P(("dp", "head"), None), P("dp", "head"), P("head", "dp")),
        check_vma=False,
    )
```

profile of v0, /device:TPU:0, one launch (start us, length us, event | category | flops | bytes accessed | tf_op | source)
XLA Modules:
  0.0 126.2 jit_solution(11984738553274445787)
XLA Ops:
  0.6 0.7 convert_multiply_fusion
  1.3 0.7 broadcast_in_dim.3
  2.0 112.6 %shard_map.76 = (bf16[32,8192]{1,0:T(8,128)(2,1)}, bf16[4,2,32,1024]{3,2,1,0:T(8,128)(2,1)}, f32[1024,2048]{1,0:T(8,128)}) custom-call(bf16[256,1024]{1,0:T(8,128)(2,1)} %attn.1, f32[1,1024]{1,0:T(1,128)} %bitcast.3, bf16[32,8192]{1,0:T(8,128)(2,1)} %grad.1, bf16[1024,2048]{1,0:T(8,128)(2,1)} %w_hbm.1), custom_call_target="tpu_custom_call" | custom-call | tf_op jit(solution)/shard_map/pallas_call | solution.py:248
  114.6 1.9 %copy.11 = bf16[32,8192]{1,0:T(8,128)(2,1)} copy(bf16[32,8192]{1,0:T(8,128)(2,1)} %get-tuple-element.12) | data formatting | bytes 1048576
  116.4 1.9 %copy.12 = bf16[256,1024]{1,0:T(8,128)(2,1)} copy(bf16[256,1024]{1,0:T(8,128)(2,1)} %bitcast.2) | data formatting | bytes 1048576
  118.3 7.9 %copy.13 = f32[1024,2048]{1,0:T(8,128)} copy(f32[1024,2048]{1,0:T(8,128)} %get-tuple-element.14) | data formatting | bytes 16777216
where the time goes:
time: 127 us; the launch traced here: 126 us
  Pallas kernels  113 us (89%)
  local copies, waits for them, and re-layouts  12.3 us (10%)
    pallas_call x1, Pallas kernels, fused(): pl.pallas_call(functools.partial(kernel, nh, nd), out_shape=(jax.ShapeDty...  113 us
    unnamed x3, local copies, waits for them, and re-layouts  11.6 us

commit v1 on v0

v1 whole, which is shorter than its diff:
```python
import functools

import jax
import jax.numpy as jnp
from jax import lax
from jax.experimental import pallas as pl
from jax.experimental.pallas import tpu as pltpu
from jax.sharding import PartitionSpec as P

MESH = pl.DeviceIdType.MESH
F32, BF16 = jnp.float32, jnp.bfloat16
TILE = 256
SHARE = 5, 8
VMEM_LIMIT = 62 * 1024 * 1024


def split(cols):
    tiles = cols // TILE
    return max(1, min(tiles - 1, tiles * SHARE[0] // SHARE[1])) * TILE


def kernel(nh, nd, attn, mask, scale, grad, w_hbm, pj_hbm, ga_hbm, gt_hbm, g_hbm,
           gate, blocks, gated, gt, w, g, p0, p1, psy, ry, sz1, sz2, rz1, rz2, fb, ryf, fin, pj,
           bs, bo, br, bs2, br2, ga, ssem, rsem, lsem):
    na, nx = nh // 2, nd // 2
    h, d = lax.axis_index("head"), lax.axis_index("dp")
    z, b = h // 2, h % 2
    x, c = d // 2, d % 2
    rows, cols = g.shape[-2:]
    width = attn.shape[1]
    cut = split(cols)
    first, rest = pl.ds(0, cut), pl.ds(cut, cols - cut)
    sent = []
    ids = {}

    def when(cond, fn):
        if cond is None:
            fn()
        else:
            pl.when(cond)(fn)

    def slot(key):
        return ids.setdefault(key, len(ids))

    def remote(key, src, dst, dev):
        i = slot(key)
        return pltpu.make_async_remote_copy(
            src_ref=src, dst_ref=dst, send_sem=ssem.at[i], recv_sem=rsem.at[i],
            device_id=dev, device_id_type=MESH,
        )

    def send(key, cond, make, dev):
        when(cond, lambda: remote(key, *make(), dev).start())
        sent.append((key, cond, make, dev))

    def arrive(key, ref, dev):
        remote(key, ref, ref, dev).wait_recv()

    def dp(q):
        return {"head": h, "dp": q}

    def along(step):
        return {"head": (h + 2 * step + nh) % nh, "dp": d}

    beside = {"head": z * 2 + 1 - b, "dp": d}
    sibling = dp(x * 2 + 1 - c)

    def ahead(s):
        return ((x + s[0]) % nx) * 2 + (c + s[1]) % 2

    def behind(s):
        return ((x + nx - s[0]) % nx) * 2 + (c + s[1]) % 2

    far = [(kx, kc) for kx in range(1, nx) for kc in range(2)]

    def part(q):
        return grad.at[:, pl.ds(pl.multiple_of(q * cols, 128), cols)]

    w_copy = pltpu.make_async_copy(w_hbm, w, lsem.at[0])
    w_copy.start()
    own_copy = pltpu.make_async_copy(part(d), g.at[0, 0, z, 0], lsem.at[1])
    own_copy.start()

    heads = scale.shape[0]
    each = width // heads
    for i in range(heads):
        gate[:, i * each:(i + 1) * each] = jnp.full((1, each), mask[i].astype(F32) * scale[i], F32)

    barrier = pltpu.get_barrier_semaphore()

    def greet(dev):
        pl.semaphore_signal(barrier, inc=1, device_id=dev, device_id_type=MESH)

    for s in far + [(0, 1)]:
        greet(dp(ahead(s)))
    greet(beside)
    pl.when(z > 0)(lambda: greet(along(-1)))
    pl.when(z < na - 1)(lambda: greet(along(1)))
    pl.semaphore_wait(barrier, nd + (z + na - 1) // na + (2 * na - 2 - z) // na)

    for s in far + [(0, 1)]:
        send(("swap", s), None, lambda s=s: (part(ahead(s)), g.at[0, s[0], z, s[1]]), dp(ahead(s)))
    for k in range(1, nx):
        send(("attn", k), None, lambda k=k: (attn, blocks.at[k, 0]), dp(ahead((k, 0))))
    send(("attn", 0), None, lambda: (attn, blocks.at[0, 1]), sibling)

    def swapped(s):
        arrive(("swap", s), g.at[0, s[0], z, s[1]], dp(behind(s)))

    RIGHT, LEFT = 0, 1
    both = (RIGHT, LEFT)

    def unit(p, way):
        return z - p if way == RIGHT else z + p

    def held(p, way):
        return z >= p if way == RIGHT else z + p <= na - 1

    def open_to(way):
        return z < na - 1 if way == RIGHT else z > 0

    def open_from(way):
        return z > 0 if way == RIGHT else z < na - 1

    def step(way):
        return 1 if way == RIGHT else -1

    def ref_z(p, k, way, piece):
        u = unit(p, way)
        return g.at[0, k, u] if piece == 0 else g.at[1, k, u, :, :, rest]

    def gather_z(p, k, piece):
        for way in both:
            def make(way=way):
                ref = ref_z(p, k, way, piece)
                return ref, ref
            send(("gz", p, k, way, piece), held(p, way) & open_to(way), make, along(step(way)))

    def gathered_z(p, k, piece):
        for way in both:
            def wait(way=way):
                arrive(("gz", p - 1, k, way, piece), ref_z(p, k, way, piece), along(-step(way)))
            when(held(p, way), wait)

    def ref_y(p, k, way, r):
        return g.at[r, k, z] if p == 0 else g.at[r, k, unit(p, way), :, :, first]

    def gather_y(p, k):
        for way in both[:1] if p == 0 else both:
            def make(way=way):
                return ref_y(p, k, way, 0), ref_y(p, k, way, 1)
            send(("gy", p, k, way), None if p == 0 else held(p, way), make, beside)

    def gathered_y(p, k):
        for way in both[:1] if p == 0 else both:
            def wait(way=way):
                arrive(("gy", p, k, way), ref_y(p, k, way, 1), beside)
            when(None if p == 0 else held(p, way), wait)

    def due(p, way):
        return p > z if way == RIGHT else p > na - 1 - z

    def target(p, way):
        return na + z - p if way == RIGHT else z + p - na

    def sum_y(p, k):
        for way in both[:1] if p == na else both:
            def make(way=way):
                t = target(p, way)
                return psy.at[k, t], ry.at[k, t]
            send(("sy", p, k, way), None if p == na else due(p, way), make, beside)

    def tiles_of(lo, hi, fn):
        @pl.loop(lo // TILE, hi // TILE)
        def _(i):
            fn(pl.ds(pl.multiple_of(i * TILE, TILE), TILE), pl.ds(pl.multiple_of(i * TILE - cut, TILE), TILE))

    def sum_z(p, k):
        for way in both:
            def run(chained, way=way):
                t = target(p, way)
                arrive(("sy", p, k, way), ry.at[k, t], beside)
                if chained:
                    arrive(("sz", p - 1, k, way, 0), rz1.at[way, k, t], along(-step(way)))

                def front(at, _):
                    val = p0[k, t, :, :, at] + ry[k, t, :, :, at].astype(F32)
                    if chained:
                        val += rz1[way, k, t, :, :, at].astype(F32)
                    sz1[k, t, :, :, at] = val.astype(BF16)

                def back(at, _):
                    val = p0[k, t, :, :, at]
                    if chained:
                        val += rz1[way, k, t, :, :, at].astype(F32)
                    sz1[k, t, :, :, at] = val.astype(BF16)

                tiles_of(0, cut, front)
                tiles_of(cut, cols, back)

            def run2(chained, way=way):
                t = target(p, way)
                if chained:
                    arrive(("sz", p - 1, k, way, 1), rz2.at[way, k, t], along(-step(way)))

                def back(_, at):
                    val = p1[k, t, :, :, at]
                    if chained:
                        val += rz2[way, k, t, :, :, at].astype(F32)
                    sz2[k, t, :, :, at] = val.astype(BF16)

                tiles_of(cut, cols, back)

            now = due(p, way)
            for piece, fn, src, dst in ((0, run, sz1, rz1), (1, run2, sz2, rz2)):
                pl.when(now & open_from(way))(lambda fn=fn: fn(True))
                pl.when(now & jnp.logical_not(open_from(way)))(lambda fn=fn: fn(False))

                def make(way=way, src=src, dst=dst):
                    t = target(p, way)
                    return src.at[k, t], dst.at[way, k, t]
                send(("sz", p, k, way, piece), now, make, along(step(way)))

    def phase(p, k):
        gathered_z(p, k, 0)
        gather_z(p, k, 0)
        gather_y(p, k)
        sum_z(p, k)
        gathered_z(p, k, 1)
        gather_z(p, k, 1)
        sum_y(p + 1, k)

    def put(val, kx, kc):
        val = (val.astype(F32) * gate[...]).astype(BF16).reshape(na, 2, rows, width)
        for bb in range(2):
            gated[(b + bb) % 2, kx, :, kc] = val[:, bb]

    def turn(k):
        span = na * 2 * rows
        for r in range(2):
            lo = (r * nx + k) * span
            gt[:, lo:lo + span] = gated[r, k].reshape(span, width).T

    def project(k):
        def dot(at):
            lhs = gated[:, k].reshape(2 * na * 2 * rows, width)
            res = jnp.dot(lhs, w[:, at], preferred_element_type=F32)
            return res.reshape(2, na, 2, rows, TILE)

        def front(at, _):
            res = dot(at)
            p0[k, :, :, :, at] = res[0]
            psy[k, :, :, :, at] = res[1].astype(BF16)

        def back(at, low):
            res = dot(at)
            p0[k, :, :, :, at] = res[0]
            p1[k, :, :, :, low] = res[1]

        tiles_of(0, cut, front)
        tiles_of(cut, cols, back)

    small = jnp.minimum(z, na - 1 - z)

    def nth(j):
        if j == 0:
            return z
        near = z - (j + 1) // 2 if j % 2 else z + (j + 1) // 2
        end = jnp.where(z == small, j, na - 1 - j)
        return jnp.where(j <= 2 * small, near, end)

    def back(j):
        u = nth(j)
        if j:
            for k in range(nx):
                gathered_y(j, k)

        @pl.loop(0, width // TILE)
        def _(t):
            at = pl.ds(pl.multiple_of(t * TILE, TILE), TILE)
            lhs = g[:, :, u].reshape(2 * nx * 2 * rows, cols)
            res = lax.dot_general(lhs, w[at, :], (((1,), (1,)), ((), ())), preferred_element_type=F32)
            res = res.reshape(2, nx, 2, rows, TILE)
            bs[j, :, :, :, at] = res[:, :, 1].astype(BF16)
            bo[j, :, :, :, at] = res[:, :, 0]

        send(("pair", j), None, lambda: (bs.at[j], br.at[j]), sibling)

    def cross(j):
        arrive(("pair", j), br.at[j], sibling)
        for k in range(1, nx):
            bs2[j, k - 1] = (bo[j, :, k] + br[j, :, k].astype(F32)).astype(BF16)
            send(("cross", j, k), None, lambda k=k: (bs2.at[j, k - 1], br2.at[j, k - 1]), dp(behind((k, 0))))

    own_copy.wait()
    swapped((0, 1))
    gather_z(0, 0, 0)
    gather_y(0, 0)
    put(attn[...], 0, 0)
    arrive(("attn", 0), blocks.at[0, 1], sibling)
    put(blocks[0, 1], 0, 1)
    w_copy.wait()
    project(0)
    for k in range(1, nx):
        for kc in range(2):
            swapped((k, kc))
        gather_z(0, k, 0)
        gather_y(0, k)
    gathered_y(0, 0)
    gather_z(0, 0, 1)
    sum_y(1, 0)
    phase(1, 0)
    turn(0)
    for k in range(1, nx):
        gathered_y(0, k)
        gather_z(0, k, 1)
    for k in range(1, nx):
        arrive(("attn", k), blocks.at[k, 0], dp(behind((k, 0))))
        send(("pass", k), None, lambda k=k: (blocks.at[k, 0], blocks.at[k, 1]), sibling)
        put(blocks[k, 0], k, 0)
    for k in range(1, nx):
        arrive(("pass", k), blocks.at[k, 1], sibling)
        put(blocks[k, 1], k, 1)
        project(k)
        sum_y(1, k)
        phase(1, k)
        turn(k)
    gt_copy = pltpu.make_async_copy(gt, gt_hbm, lsem.at[2])
    gt_copy.start()

    back(0)
    for p in range(2, na):
        for k in range(nx):
            phase(p, k)
        cross(p - 2)
        back(p - 1)
    cross(na - 2)
    back(na - 1)
    g_copy = pltpu.make_async_copy(g, g_hbm, lsem.at[3])
    g_copy.start()

    def add_in(dst, lo, piece, k, way, buf):
        def run():
            arrive(("sz", na - 1, k, way, piece), buf.at[way, k, z], along(-step(way)))

            def tile(at, low):
                at = low if piece else at
                dst[k, z, :, :, at] += buf[way, k, z, :, :, at].astype(F32)
            tiles_of(lo, cols, tile)
        pl.when(open_from(way))(run)

    for k in range(nx):
        for way in both:
            add_in(p1, cut, 1, k, way, rz2)
        fb[k] = p1[k, z].astype(BF16)
        send(("fy", k), None, lambda k=k: (fb.at[k], ryf.at[k]), beside)
    for k in range(nx):
        for way in both:
            add_in(p0, 0, 0, k, way, rz1)
    cross(na - 1)

    def finish(k):
        arrive(("sy", na, k, RIGHT), ry.at[k, z], beside)

        def front(at, _):
            fin[k, :, :, at] = (p0[k, z, :, :, at] + ry[k, z, :, :, at].astype(F32)).astype(BF16)

        tiles_of(0, cut, front)
        arrive(("fy", k), ryf.at[k], beside)

        def rear(at, low):
            fin[k, :, :, at] = (p0[k, z, :, :, at] + ryf[k, :, :, low].astype(F32)).astype(BF16)

        tiles_of(cut, cols, rear)
        for kc in range(2):
            if (k, kc) != (0, 0):
                send(("home", (k, kc)), None, lambda kc=kc: (fin.at[k, kc], pj.at[d]), dp(behind((k, kc))))

    for k in list(range(1, nx)) + [0]:
        finish(k)
    pj[d] = fin[0, 0]

    for j in range(na):
        for k in range(1, nx):
            arrive(("cross", j, k), br2.at[j, k - 1], dp(ahead((k, 0))))
        total = bo[j, :, 0] + br[j, :, 0].astype(F32)
        for k in range(1, nx):
            total += br2[j, k - 1].astype(F32)
        total = (total * gate[...].reshape(1, 1, width)).astype(BF16)
        for r in range(2):
            ga[nth(j), (b + r) % 2] = total[r]
    ga_copy = pltpu.make_async_copy(ga, ga_hbm, lsem.at[4])
    ga_copy.start()
    for s in [(0, 1)] + far:
        arrive(("home", s), pj.at[ahead(s)], dp(ahead(s)))
    pj_copy = pltpu.make_async_copy(pj, pj_hbm, lsem.at[5])
    pj_copy.start()
    for key, cond, make, dev in sent:
        when(cond, lambda: remote(key, *make(), dev).wait_send())
    gt_copy.wait()
    g_copy.wait()
    ga_copy.wait()
    pj_copy.wait()


def weight_kernel(gt, g, pj, ga, gw, proj, gattn):
    width = gt.shape[0]

    @pl.loop(0, width // TILE)
    def _(t):
        at = pl.ds(pl.multiple_of(t * TILE, TILE), TILE)
        gw[at, :] = jnp.dot(gt[at, :], g[...], preferred_element_type=F32)

    proj[...] = pj[0]
    gattn[...] = ga[...]


def fused(nh, nd, attn_out, head_mask, gate_scale, w_out, grad_out):
    na, nx = nh // 2, nd // 2
    rows, cols, width = grad_out.shape[0], w_out.shape[1], w_out.shape[0]
    tokens = rows * nh * nd
    cut = split(cols)
    n_sems = 2 * nd + 4 * nx + 11 * (na + 1) * nx * 2 + na * nx
    vmem = pl.BlockSpec(memory_space=pltpu.VMEM)
    smem = pl.BlockSpec(memory_space=pltpu.SMEM)
    hbm = pl.BlockSpec(memory_space=pl.ANY)
    order = (2, nx, na, 2, rows)
    half = (nx, na, 2, rows)
    pj, ga, gt, g = pl.pallas_call(
        functools.partial(kernel, nh, nd),
        out_shape=(
            jax.ShapeDtypeStruct((nd, rows, cols), BF16),
            jax.ShapeDtypeStruct((na, 2, rows, width), BF16),
            jax.ShapeDtypeStruct((width, tokens), BF16),
            jax.ShapeDtypeStruct(order + (cols,), BF16),
        ),
        in_specs=[vmem, smem, smem, vmem, hbm],
        out_specs=(hbm, hbm, hbm, hbm),
        scratch_shapes=[
            pltpu.VMEM((1, width), F32),
            pltpu.VMEM((nx, 2, nh * rows, width), BF16),
            pltpu.VMEM(order + (width,), BF16),
            pltpu.VMEM((width, tokens), BF16),
            pltpu.VMEM(w_out.shape, BF16),
            pltpu.VMEM(order + (cols,), BF16),
            pltpu.VMEM(half + (cols,), F32),
            pltpu.VMEM(half + (cols - cut,), F32),
            pltpu.VMEM(half + (cut,), BF16),
            pltpu.VMEM(half + (cut,), BF16),
            pltpu.VMEM(half + (cols,), BF16),
            pltpu.VMEM(half + (cols - cut,), BF16),
            pltpu.VMEM((2,) + half + (cols,), BF16),
            pltpu.VMEM((2,) + half + (cols - cut,), BF16),
            pltpu.VMEM((nx, 2, rows, cols - cut), BF16),
            pltpu.VMEM((nx, 2, rows, cols - cut), BF16),
            pltpu.VMEM((nx, 2, rows, cols), BF16),
            pltpu.VMEM((nd, rows, cols), BF16),
            pltpu.VMEM((na, 2, nx, rows, width), BF16),
            pltpu.VMEM((na, 2, nx, rows, width), F32),
            pltpu.VMEM((na, 2, nx, rows, width), BF16),
            pltpu.VMEM((na, nx - 1, 2, rows, width), BF16),
            pltpu.VMEM((na, nx - 1, 2, rows, width), BF16),
            pltpu.VMEM((na, 2, rows, width), BF16),
            pltpu.SemaphoreType.DMA((n_sems,)),
            pltpu.SemaphoreType.DMA((n_sems,)),
            pltpu.SemaphoreType.DMA((6,)),
        ],
        compiler_params=pltpu.CompilerParams(
            collective_id=0, has_side_effects=True, vmem_limit_bytes=VMEM_LIMIT
        ),
    )(attn_out, head_mask, gate_scale, grad_out, w_out)
    each = tokens // nd // nd
    gw, proj, gattn = pl.pallas_call(
        weight_kernel,
        grid=(nd,),
        out_shape=(
            jax.ShapeDtypeStruct(w_out.shape, F32),
            jax.ShapeDtypeStruct(grad_out.shape, BF16),
            jax.ShapeDtypeStruct(attn_out.shape, BF16),
        ),
        in_specs=[
            pl.BlockSpec((width, tokens), lambda i: (0, 0)),
            pl.BlockSpec((tokens, cols // nd), lambda i: (0, i)),
            pl.BlockSpec((1, rows, cols), lambda i: (i, 0, 0)),
            pl.BlockSpec((each, width), lambda i: (i, 0)),
        ],
        out_specs=(
            pl.BlockSpec((width, cols // nd), lambda i: (0, i)),
            pl.BlockSpec((rows, cols), lambda i: (0, i)),
            pl.BlockSpec((each, width), lambda i: (i, 0)),
        ),
        compiler_params=pltpu.CompilerParams(vmem_limit_bytes=VMEM_LIMIT // 2),
    )(gt, g.reshape(tokens, cols), pj, ga.reshape(attn_out.shape))
    return proj, gattn, gw


def shards(attn_out, head_mask, gate_scale, w_out, grad_out):
    n_dp, n_head = lax.axis_size("dp"), lax.axis_size("head")
    rows, (width, cols) = grad_out.shape[0], w_out.shape
    if rows % 16 == 0 and n_dp % 2 == 0 and n_head % 2 == 0 and min(n_dp, n_head) > 2 and width % TILE == 0 and cols % (2 * TILE) == 0 and cols % (n_dp * 128) == 0 and (width // head_mask.shape[0]) % 128 == 0 and n_head * rows % n_dp == 0:
        return fused(n_head, n_dp, attn_out, head_mask, gate_scale, w_out, grad_out)
    gate_vals = head_mask.astype(jnp.float32) * gate_scale
    width_each = attn_out.shape[1] // gate_vals.shape[0]
    col_gate = jnp.repeat(gate_vals, width_each)
    gated = (attn_out.astype(jnp.float32) * col_gate[None, :]).astype(jnp.bfloat16)
    mine = lax.all_to_all(grad_out, "dp", 1, 0, tiled=True)
    every = lax.all_gather(mine.reshape(n_dp, rows, cols), "head", axis=1)
    grad_cols = every.reshape(n_dp * n_head * rows, cols)
    gated_all = lax.all_gather(gated, "dp", axis=0, tiled=True)
    part = jnp.dot(gated_all, w_out, preferred_element_type=jnp.float32).astype(jnp.bfloat16)
    summed = lax.psum_scatter(part.reshape(n_dp, n_head, rows, cols), "head", scatter_dimension=1, tiled=False)
    proj_out = lax.all_to_all(summed.reshape(n_dp * rows, cols), "dp", 0, 1, tiled=True)
    back = lax.dot_general(grad_cols, w_out, (((1,), (1,)), ((), ())), preferred_element_type=jnp.float32)
    back = lax.psum_scatter(back.astype(jnp.bfloat16), "dp", scatter_dimension=0, tiled=True)
    grad_attn = (back.astype(jnp.float32) * col_gate[None, :]).astype(jnp.bfloat16)
    grad_w = lax.dot_general(gated_all, grad_cols, (((0,), (0,)), ((), ())), preferred_element_type=jnp.float32)
    return (proj_out, grad_attn, grad_w)


def solution(mesh):
    return jax.shard_map(
        shards,
        mesh=mesh,
        in_specs=(P("dp", "head"), P("head"), P("head"), P("head", "dp"), P(("dp", "head"), None)),
        out_specs=(P(("dp", "head"), None), P("dp", "head"), P("head", "dp")),
        check_vma=False,
    )
```

time: 127 us -> 103 us (0.81)
  Pallas kernels: 113 us -> 95.2 us
  local copies, waits for them, and re-layouts: 12.3 us -> 5.85 us
    pallas_call x1, Pallas kernels: 113 us -> 86.4 us  [fused(): pl.pallas_call(functools.partial(kernel, nh, nd), out_shape=(jax.ShapeDty...]
    pallas_call x0 -> x1, Pallas kernels: none -> 8.8 us  [fused(): pl.pallas_call(weight_kernel, grid=(nd,), out_shape=(jax.ShapeDtypeStruct...]
    unnamed x3 -> x8, local copies, waits for them, and re-layouts: 11.6 us -> 5.85 us
where the time goes in v1:
time: 103 us; the launch traced here: 102 us
  Pallas kernels  95.2 us (92%)
  local copies, waits for them, and re-layouts  5.85 us (6%)
    pallas_call x1, Pallas kernels, fused(): pl.pallas_call(functools.partial(kernel, nh, nd), out_shape=(jax.ShapeDty...  86.4 us
    pallas_call x1, Pallas kernels, fused(): pl.pallas_call(weight_kernel, grid=(nd,), out_shape=(jax.ShapeDtypeStruct...  8.8 us
    unnamed x8, local copies, waits for them, and re-layouts  5.85 us

profile of v1, /device:TPU:0, one launch (start us, length us, event | category | flops | bytes accessed | tf_op | source)
XLA Modules:
  0.0 101.8 jit_solution(13725329757284077197)
XLA Ops:
  0.6 86.4 %shard_map.76 = (bf16[4,32,2048]{2,1,0:T(8,128)(2,1)}, bf16[4,2,32,1024]{3,2,1,0:T(8,128)(2,1)}, bf16[1024,1024]{1,0:T(8,128)(2,1)}, bf16[2,2,4,2,32,2048]{5,4,3,2,1,0:T(8,128)(2,1)}) custom-call(bf16[256,1024]{1,0:T(8,128)(2,1)} %attn.1, s32[8]{0:T(128)} %mask.1, f32[8]{0:T(128)} %scale.1, bf16[32,8192]{1,0:T(8,128)(2,1)} %grad.1, bf16[1024,2048]{1,0:T(8,128)(2,1)} %w_hbm.1), custom_call_target="tpu_custom_call" | custom-call | tf_op jit(solution)/shard_map/pallas_call | solution.py:429
  87.1 0.0 copy-start
  87.1 2.2 %copy-done = bf16[2,2,4,2,32,2048]{5,4,3,2,1,0:T(8,128)(2,1)S(1)} copy-done((bf16[2,2,4,2,32,2048]{5,4,3,2,1,0:T(8,128)(2,1)S(1)}, bf16[2,2,4,2,32,2048]{5,4,3,2,1,0:T(8,128)(2,1)}, u32[]{:S(2)}) %copy-start) | copy-done | bytes 4194328
  89.3 0.0 copy-start.1
  89.3 1.6 %copy-done.1 = bf16[1024,1024]{1,0:T(8,128)(2,1)S(1)} copy-done((bf16[1024,1024]{1,0:T(8,128)(2,1)S(1)}, bf16[1024,1024]{1,0:T(8,128)(2,1)}, u32[]{:S(2)}) %copy-start.1) | copy-done | bytes 2097176
  90.9 0.0 copy-start.2
  90.9 1.0 %copy-done.2 = bf16[4,32,2048]{2,1,0:T(8,128)(2,1)S(1)} copy-done((bf16[4,32,2048]{2,1,0:T(8,128)(2,1)S(1)}, bf16[4,32,2048]{2,1,0:T(8,128)(2,1)}, u32[]{:S(2)}) %copy-start.2) | copy-done | bytes 524312
  91.9 0.0 copy-start.3
  91.9 1.0 %copy-done.3 = bf16[4,2,32,1024]{3,2,1,0:T(8,128)(2,1)S(1)} copy-done((bf16[4,2,32,1024]{3,2,1,0:T(8,128)(2,1)S(1)}, bf16[4,2,32,1024]{3,2,1,0:T(8,128)(2,1)}, u32[]{:S(2)}) %copy-start.3) | copy-done | bytes 524312
  93.0 8.8 %shard_map.77 = (f32[1024,2048]{1,0:T(8,128)}, bf16[32,8192]{1,0:T(8,128)(2,1)}, bf16[256,1024]{1,0:T(8,128)(2,1)}) custom-call(bf16[1024,1024]{1,0:T(8,128)(2,1)S(1)} %copy-done.1, bf16[1024,2048]{1,0:T(8,128)(2,1)S(1)} %bitcast.2, bf16[4,32,2048]{2,1,0:T(8,128)(2,1)S(1)} %copy-done.2, bf16[256,1024]{1,0:T(8,128)(2,1)S(1)} %bitcast.3), custom_call_target="tpu_custom_call" | custom-call | tf_op jit(solution)/shard_map/pallas_call | solution.py:473
Async XLA Ops:
  87.1 2.2 %copy-start = (bf16[2,2,4,2,32,2048]{5,4,3,2,1,0:T(8,128)(2,1)S(1)}, bf16[2,2,4,2,32,2048]{5,4,3,2,1,0:T(8,128)(2,1)}, u32[]{:S(2)}) copy-start(bf16[2,2,4,2,32,2048]{5,4,3,2,1,0:T(8,128)(2,1)} %get-tuple-element.11) | copy-start | bytes 12582916
  89.3 1.6 %copy-start.1 = (bf16[1024,1024]{1,0:T(8,128)(2,1)S(1)}, bf16[1024,1024]{1,0:T(8,128)(2,1)}, u32[]{:S(2)}) copy-start(bf16[1024,1024]{1,0:T(8,128)(2,1)} %get-tuple-element.10.gt) | copy-start | bytes 6291460
  90.9 1.0 %copy-start.2 = (bf16[4,32,2048]{2,1,0:T(8,128)(2,1)S(1)}, bf16[4,32,2048]{2,1,0:T(8,128)(2,1)}, u32[]{:S(2)}) copy-start(bf16[4,32,2048]{2,1,0:T(8,128)(2,1)} %get-tuple-element.12.pj) | copy-start | bytes 1572868
  91.9 1.0 %copy-start.3 = (bf16[4,2,32,1024]{3,2,1,0:T(8,128)(2,1)S(1)}, bf16[4,2,32,1024]{3,2,1,0:T(8,128)(2,1)}, u32[]{:S(2)}) copy-start(bf16[4,2,32,1024]{3,2,1,0:T(8,128)(2,1)} %get-tuple-element.13) | copy-start | bytes 1572868

commit v2 on v1

--- a/solution.py
+++ b/solution.py
@@ -11,7 +11,8 @@
 F32, BF16 = jnp.float32, jnp.bfloat16
 TILE = 256
 SHARE = 5, 8
-VMEM_LIMIT = 62 * 1024 * 1024
+VMEM_LIMIT = 44 * 1024 * 1024
+WEIGHT_LIMIT = 16 * 1024 * 1024
 
 
 def split(cols):
@@ -19,8 +20,8 @@
     return max(1, min(tiles - 1, tiles * SHARE[0] // SHARE[1])) * TILE
 
 
-def kernel(nh, nd, attn, mask, scale, grad, w_hbm, pj_hbm, ga_hbm, gt_hbm, g_hbm,
-           gate, blocks, gated, gt, w, g, p0, p1, psy, ry, sz1, sz2, rz1, rz2, fb, ryf, fin, pj,
+def kernel(nh, nd, attn, mask_hbm, scale_hbm, grad, w_hbm, pj_hbm, ga_hbm, gt_hbm, g_hbm,
+           mask, scale, gate, blocks, gated, gt, w, g, p0, p1, psy, ry, sz1, sz2, rz1, rz2, fb, ryf, fin, pj,
            bs, bo, br, bs2, br2, ga, ssem, rsem, lsem):
     na, nx = nh // 2, nd // 2
     h, d = lax.axis_index("head"), lax.axis_index("dp")
@@ -80,11 +81,12 @@
     w_copy.start()
     own_copy = pltpu.make_async_copy(part(d), g.at[0, 0, z, 0], lsem.at[1])
     own_copy.start()
-
-    heads = scale.shape[0]
-    each = width // heads
-    for i in range(heads):
-        gate[:, i * each:(i + 1) * each] = jnp.full((1, each), mask[i].astype(F32) * scale[i], F32)
+    mask_copy = pltpu.make_async_copy(mask_hbm, mask, lsem.at[6])
+    mask_copy.start()
+    scale_copy = pltpu.make_async_copy(scale_hbm, scale, lsem.at[7])
+    scale_copy.start()
+    attn_copy = pltpu.make_async_copy(attn, blocks.at[0, 0], lsem.at[8])
+    attn_copy.start()
 
     barrier = pltpu.get_barrier_semaphore()
 
@@ -296,7 +298,14 @@
     swapped((0, 1))
     gather_z(0, 0, 0)
     gather_y(0, 0)
-    put(attn[...], 0, 0)
+    mask_copy.wait()
+    scale_copy.wait()
+    heads = scale.shape[0]
+    each = width // heads
+    for i in range(heads):
+        gate[:, i * each:(i + 1) * each] = jnp.full((1, each), mask[i].astype(F32) * scale[i], F32)
+    attn_copy.wait()
+    put(blocks[0, 0], 0, 0)
     arrive(("attn", 0), blocks.at[0, 1], sibling)
     put(blocks[0, 1], 0, 1)
     w_copy.wait()
@@ -403,16 +412,24 @@
     pj_copy.wait()
 
 
-def weight_kernel(gt, g, pj, ga, gw, proj, gattn):
-    width = gt.shape[0]
-
-    @pl.loop(0, width // TILE)
-    def _(t):
-        at = pl.ds(pl.multiple_of(t * TILE, TILE), TILE)
-        gw[at, :] = jnp.dot(gt[at, :], g[...], preferred_element_type=F32)
-
-    proj[...] = pj[0]
-    gattn[...] = ga[...]
+def weight_kernel(gt, g, pj, ga, gw, proj, gattn, stage, osem, psem):
+    cols = g.shape[1]
+    span = stage.shape[2]
+    others = [pltpu.make_async_copy(ga, gattn, psem.at[0])]
+    for i in range(pj.shape[0]):
+        others.append(pltpu.make_async_copy(pj.at[i], proj.at[:, i * cols:(i + 1) * cols], psem.at[i + 1]))
+    for copy in others:
+        copy.start()
+    out = []
+    for i in range(cols // span):
+        slot, at = i % 2, slice(i * span, (i + 1) * span)
+        if i >= 2:
+            out[i - 2].wait()
+        stage[slot] = jnp.dot(gt[...], g[:, at], preferred_element_type=F32)
+        out.append(pltpu.make_async_copy(stage.at[slot], gw.at[:, at], osem.at[slot]))
+        out[i].start()
+    for copy in out[-2:] + others:
+        copy.wait()
 
 
 def fused(nh, nd, attn_out, head_mask, gate_scale, w_out, grad_out):
@@ -422,8 +439,8 @@
     cut = split(cols)
     n_sems = 2 * nd + 4 * nx + 11 * (na + 1) * nx * 2 + na * nx
     vmem = pl.BlockSpec(memory_space=pltpu.VMEM)
-    smem = pl.BlockSpec(memory_space=pltpu.SMEM)
-    hbm = pl.BlockSpec(memory_space=pl.ANY)
+    hbm = pl.BlockSpec(memory_space=pltpu.HBM)
+    free = pl.BlockSpec(memory_space=pl.ANY)
     order = (2, nx, na, 2, rows)
     half = (nx, na, 2, rows)
     pj, ga, gt, g = pl.pallas_call(
@@ -434,9 +451,11 @@
             jax.ShapeDtypeStruct((width, tokens), BF16),
             jax.ShapeDtypeStruct(order + (cols,), BF16),
         ),
-        in_specs=[vmem, smem, smem, vmem, hbm],
-        out_specs=(hbm, hbm, hbm, hbm),
+        in_specs=[hbm] * 5,
+        out_specs=(free,) * 4,
         scratch_shapes=[
+            pltpu.SMEM(head_mask.shape, head_mask.dtype),
+            pltpu.SMEM(gate_scale.shape, F32),
             pltpu.VMEM((1, width), F32),
             pltpu.VMEM((nx, 2, nh * rows, width), BF16),
             pltpu.VMEM(order + (width,), BF16),
@@ -463,33 +482,28 @@
             pltpu.VMEM((na, 2, rows, width), BF16),
             pltpu.SemaphoreType.DMA((n_sems,)),
             pltpu.SemaphoreType.DMA((n_sems,)),
-            pltpu.SemaphoreType.DMA((6,)),
+            pltpu.SemaphoreType.DMA((9,)),
         ],
         compiler_params=pltpu.CompilerParams(
             collective_id=0, has_side_effects=True, vmem_limit_bytes=VMEM_LIMIT
         ),
-    )(attn_out, head_mask, gate_scale, grad_out, w_out)
-    each = tokens // nd // nd
+    )(*[pltpu.with_memory_space_constraint(a, pltpu.HBM) for a in (attn_out, head_mask, gate_scale, grad_out, w_out)])
+    span = cols // nd
     gw, proj, gattn = pl.pallas_call(
         weight_kernel,
-        grid=(nd,),
         out_shape=(
             jax.ShapeDtypeStruct(w_out.shape, F32),
             jax.ShapeDtypeStruct(grad_out.shape, BF16),
             jax.ShapeDtypeStruct(attn_out.shape, BF16),
         ),
-        in_specs=[
-            pl.BlockSpec((width, tokens), lambda i: (0, 0)),
-            pl.BlockSpec((tokens, cols // nd), lambda i: (0, i)),
-            pl.BlockSpec((1, rows, cols), lambda i: (i, 0, 0)),
-            pl.BlockSpec((each, width), lambda i: (i, 0)),
+        in_specs=[vmem] * 4,
+        out_specs=(hbm,) * 3,
+        scratch_shapes=[
+            pltpu.VMEM((2, width, span), F32),
+            pltpu.SemaphoreType.DMA((2,)),
+            pltpu.SemaphoreType.DMA((nd + 1,)),
         ],
-        out_specs=(
-            pl.BlockSpec((width, cols // nd), lambda i: (0, i)),
-            pl.BlockSpec((rows, cols), lambda i: (0, i)),
-            pl.BlockSpec((each, width), lambda i: (i, 0)),
-        ),
-        compiler_params=pltpu.CompilerParams(vmem_limit_bytes=VMEM_LIMIT // 2),
+        compiler_params=pltpu.CompilerParams(vmem_limit_bytes=WEIGHT_LIMIT),
     )(gt, g.reshape(tokens, cols), pj, ga.reshape(attn_out.shape))
     return proj, gattn, gw
 
@@ -497,7 +511,7 @@
 def shards(attn_out, head_mask, gate_scale, w_out, grad_out):
     n_dp, n_head = lax.axis_size("dp"), lax.axis_size("head")
     rows, (width, cols) = grad_out.shape[0], w_out.shape
-    if rows % 16 == 0 and n_dp % 2 == 0 and n_head % 2 == 0 and min(n_dp, n_head) > 2 and width % TILE == 0 and cols % (2 * TILE) == 0 and cols % (n_dp * 128) == 0 and (width // head_mask.shape[0]) % 128 == 0 and n_head * rows % n_dp == 0:
+    if rows % 16 == 0 and n_dp % 2 == 0 and n_head % 2 == 0 and min(n_dp, n_head) > 2 and width % TILE == 0 and cols % (2 * TILE) == 0 and cols % (n_dp * 128) == 0 and (width // head_mask.shape[0]) % 128 == 0:
         return fused(n_head, n_dp, attn_out, head_mask, gate_scale, w_out, grad_out)
     gate_vals = head_mask.astype(jnp.float32) * gate_scale
     width_each = attn_out.shape[1] // gate_vals.shape[0]

time: 103 us -> 93.4 us (0.907)
  local copies, waits for them, and re-layouts: 5.85 us -> 0 us
  Pallas kernels: 95.2 us -> 91.3 us
    unnamed x8 -> x0, local copies, waits for them, and re-layouts: 5.85 us -> none
    pallas_call x1, Pallas kernels: 8.8 us -> 6.46 us  [fused(): pl.pallas_call(weight_kernel, out_shape=(jax.ShapeDtypeStruct(w_out.shape...]
    pallas_call x1, Pallas kernels: 86.4 us -> 84.8 us  [fused(): pl.pallas_call(functools.partial(kernel, nh, nd), out_shape=(jax.ShapeDty...]
where the time goes in v2:
time: 93.4 us; the launch traced here: 91.9 us
  Pallas kernels  91.3 us (98%)
    pallas_call x1, Pallas kernels, fused(): pl.pallas_call(functools.partial(kernel, nh, nd), out_shape=(jax.ShapeDty...  84.8 us
    pallas_call x1, Pallas kernels, fused(): pl.pallas_call(weight_kernel, out_shape=(jax.ShapeDtypeStruct(w_out.shape...  6.46 us

profile of v2, /device:TPU:0, one launch (start us, length us, event | category | flops | bytes accessed | tf_op | source)
XLA Modules:
  0.0 91.9 jit_solution(2526829527298242468)
XLA Ops:
  0.6 84.8 %shard_map.76 = (bf16[4,32,2048]{2,1,0:T(8,128)(2,1)S(1)}, bf16[4,2,32,1024]{3,2,1,0:T(8,128)(2,1)S(1)}, bf16[1024,1024]{1,0:T(8,128)(2,1)S(1)}, bf16[2,2,4,2,32,2048]{5,4,3,2,1,0:T(8,128)(2,1)S(1)}) custom-call(bf16[256,1024]{1,0:T(8,128)(2,1)} %attn.1, s32[8]{0:T(128)} %mask_hbm.1, f32[8]{0:T(128)} %scale_hbm.1, bf16[32,8192]{1,0:T(8,128)(2,1)} %grad.1, ...), custom_call_target="tpu_custom_call" | custom-call | tf_op jit(solution)/shard_map/pallas_call | solution.py:446
  85.5 6.5 %shard_map.77 = (f32[1024,2048]{1,0:T(8,128)}, bf16[32,8192]{1,0:T(8,128)(2,1)}, bf16[256,1024]{1,0:T(8,128)(2,1)}) custom-call(bf16[1024,1024]{1,0:T(8,128)(2,1)S(1)} %get-tuple-element.10.gt, bf16[1024,2048]{1,0:T(8,128)(2,1)S(1)} %bitcast.2, bf16[4,32,2048]{2,1,0:T(8,128)(2,1)S(1)} %get-tuple-element.12.pj, bf16[256,1024]{1,0:T(8,128)(2,1)S(1)} %bitcast.3), custom_call_target="tpu_custom_call" | custom-call | tf_op jit(solution)/shard_map/pallas_call | solution.py:492

commit v3 on v2

v3 whole, which is shorter than its diff:
```python
import functools

import jax
import jax.numpy as jnp
from jax import lax
from jax.experimental import pallas as pl
from jax.experimental.pallas import tpu as pltpu
from jax.sharding import PartitionSpec as P

MESH = pl.DeviceIdType.MESH
F32, BF16 = jnp.float32, jnp.bfloat16
TILE = 256
SHARE = 5, 8
VMEM_LIMIT = 41 * 1024 * 1024
HAND_LIMIT = 2 * 1024 * 1024
SLOTS = 3


ORDER = (
    ("gy", 0, 0), ("gz", 0, 0, 0), ("put", 0), ("proj", 0), ("sy", 2, 0), ("turn", 0), ("sb", 1, 0),
    ("gy", 0, 1), ("gz", 0, 1, 0), ("gz", 1, 0, 0), ("sy", 1, 0), ("gz", 0, 0, 1), ("gy", 1, 0), ("sb", 2, 0),
    ("gy", 1, 1), ("pass", 1), ("gz", 0, 1, 1), ("gy", 2, 0), ("gz", 1, 1, 0), ("put", 1), ("gz", 1, 0, 1),
    ("gz", 2, 0, 0), ("proj", 1), ("sb", 1, 1), ("sb", 2, 1), ("sy", 2, 1), ("gz", 2, 1, 0), ("gz", 1, 1, 1),
    ("sa", 1, 0), ("back", 1), ("sy", 1, 1), ("gy", 2, 1), ("sa", 1, 1), ("turn", 1), ("sy", 3, 1),
    ("sb", 3, 1), ("gy", 3, 0), ("cross", 1), ("back", 0), ("sa", 2, 1), ("gy", 3, 1), ("gz", 2, 0, 1),
    ("back", 2), ("ga", 1), ("sy", 3, 0), ("cross", 2), ("cross", 0), ("gz", 2, 1, 1), ("fb", 1),
    ("sy", 4, 1), ("sa", 2, 0), ("sa", 3, 1), ("sb", 3, 0), ("back", 3), ("gw", 6), ("sy", 4, 0),
    ("sa", 3, 0), ("cross", 3), ("gw", 3), ("gw", 4), ("ga", 2), ("fa", 1), ("fin", 1), ("gw", 1), ("fb", 0),
    ("ga", 0), ("gw", 5), ("gw", 2), ("ga", 3), ("gw", 7), ("fa", 0), ("fin", 0), ("gw", 0),
)


def split(cols):
    tiles = cols // TILE
    return max(1, min(tiles - 1, tiles * SHARE[0] // SHARE[1])) * TILE


def plan(na, nx, tiles):
    order = [("gz", 0, 0, 0), ("gy", 0, 0), ("put", 0), ("proj", 0)]
    for k in range(1, nx):
        order += [("gz", 0, k, 0), ("gy", 0, k)]
    order += [("gz", 0, 0, 1), ("sy", 1, 0), ("turn", 0)]
    for k in range(1, nx):
        order += [("gz", 0, k, 1), ("pass", k)]
    for k in range(1, nx):
        order += [("put", k), ("proj", k), ("sy", 1, k), ("turn", k)]
    for p in range(1, na):
        for k in range(nx):
            order += [("gz", p, k, 0)] if p < na - 1 else []
            order += [("gy", p, k), ("sb", p, k)]
            order += [("gz", p, k, 1)] if p < na - 1 else []
            order += [("sa", p, k), ("sy", p + 1, k)]
        order += [("cross", p - 2)] if p > 1 else []
        order += [("back", p - 1)]
    order += [("cross", na - 2), ("back", na - 1)]
    order += [("fb", k) for k in range(nx)] + [("fa", k) for k in range(nx)] + [("cross", na - 1)]
    order += [("fin", k) for k in reversed(range(nx))]
    order += [("gw", i) for i in range(tiles)] + [("ga", j) for j in range(na)]
    return ORDER if set(ORDER) == set(order) else order


def kernel(nh, nd, attn, mask_hbm, scale_hbm, grad, w_hbm, pj_out, ga_out, *more):
    gw_outs, more = more[:nd], more[nd:]
    (mask, scale, gate, blocks, gated, gt, w, g, pa, pb, psy, ry, sa, sb, ra, rb, fb, ryf, fin, pj,
     bs, bo, br, bs2, br2, ga, gw, ssem, rsem, lsem) = more
    na, nx = nh // 2, nd // 2
    h, d = lax.axis_index("head"), lax.axis_index("dp")
    z, b = h // 2, h % 2
    x, c = d // 2, d % 2
    rows, cols = g.shape[-2:]
    width, tokens = gt.shape
    cut = split(cols)
    first, rest = pl.ds(0, cut), pl.ds(cut, cols - cut)
    sent, ids, seen = [], {}, set()
    local, tiles = [], []

    def when(cond, fn):
        if cond is None:
            fn()
        else:
            pl.when(cond)(fn)

    def remote(key, src, dst, dev):
        i = ids.setdefault(key, len(ids))
        return pltpu.make_async_remote_copy(
            src_ref=src, dst_ref=dst, send_sem=ssem.at[i], recv_sem=rsem.at[i],
            device_id=dev, device_id_type=MESH,
        )

    def send(key, cond, make, dev):
        when(cond, lambda: remote(key, *make(), dev).start())
        sent.append((key, cond, make, dev))

    def arrive(key, ref, dev):
        remote(key, ref, ref, dev).wait_recv()

    def once(key, cond, make, dev):
        if key not in seen:
            seen.add(key)
            when(cond, lambda: arrive(key, make(), dev))

    def copy(src, dst):
        made = pltpu.make_async_copy(src, dst, lsem.at[len(local)])
        made.start()
        local.append(made)
        return len(local) - 1

    def copied(i):
        if local[i] is not None:
            local[i].wait()
            local[i] = None

    def dp(q):
        return {"head": h, "dp": q}

    def along(step):
        return {"head": (h + 2 * step + nh) % nh, "dp": d}

    beside = {"head": z * 2 + 1 - b, "dp": d}
    sibling = dp(x * 2 + 1 - c)

    def ahead(s):
        return ((x + s[0]) % nx) * 2 + (c + s[1]) % 2

    def behind(s):
        return ((x + nx - s[0]) % nx) * 2 + (c + s[1]) % 2

    far = [(kx, kc) for kx in range(1, nx) for kc in range(2)]

    def part(q):
        return grad.at[:, pl.ds(pl.multiple_of(q * cols, 128), cols)]

    own_copy = copy(part(d), g.at[0, 0, z, 0])
    attn_copy = copy(attn, blocks.at[0, 0])
    mask_copy = copy(mask_hbm, mask)
    scale_copy = copy(scale_hbm, scale)
    w_copy = copy(w_hbm, w)
    barrier = pltpu.get_barrier_semaphore()

    def greet(dev):
        pl.semaphore_signal(barrier, inc=1, device_id=dev, device_id_type=MESH)

    for s in far + [(0, 1)]:
        greet(dp(ahead(s)))
    greet(beside)
    pl.when(z > 0)(lambda: greet(along(-1)))
    pl.when(z < na - 1)(lambda: greet(along(1)))
    pl.semaphore_wait(barrier, nd + (z + na - 1) // na + (2 * na - 2 - z) // na)

    for s in far + [(0, 1)]:
        send(("swap", s), None, lambda s=s: (part(ahead(s)), g.at[0, s[0], z, s[1]]), dp(ahead(s)))
    for k in range(1, nx):
        send(("attn", k), None, lambda k=k: (attn, blocks.at[k, 0]), dp(ahead((k, 0))))
    send(("attn", 0), None, lambda: (attn, blocks.at[0, 1]), sibling)

    both = RIGHT, LEFT = 0, 1

    def unit(p, way):
        return z - p if way == RIGHT else z + p

    def held(p, way):
        return z >= p if way == RIGHT else z + p <= na - 1

    def open_to(way):
        return z < na - 1 if way == RIGHT else z > 0

    def open_from(way):
        return z > 0 if way == RIGHT else z < na - 1

    def step(way):
        return 1 if way == RIGHT else -1

    def due(p, way):
        return p > z if way == RIGHT else p > na - 1 - z

    def target(p, way):
        return na + z - p if way == RIGHT else z + p - na

    def ref_z(p, k, way, piece):
        u = unit(p, way)
        return g.at[0, k, u] if piece == 0 else g.at[1, k, u, :, :, rest]

    def ref_y(p, k, way, r):
        return g.at[r, k, z] if p == 0 else g.at[r, k, unit(p, way), :, :, first]

    def need_z(p, k, piece):
        if p:
            for way in both:
                once(("gz", p - 1, k, way, piece), held(p, way), lambda way=way: ref_z(p, k, way, piece), along(-step(way)))
        elif piece:
            need_y(0, k)
        else:
            for s in ((k, 0), (k, 1)):
                if s == (0, 0):
                    copied(own_copy)
                else:
                    once(("swap", s), None, lambda s=s: g.at[0, s[0], z, s[1]], dp(behind(s)))

    def need_y(p, k):
        for way in both if p else both[:1]:
            once(("gy", p, k, way), held(p, way) if p else None, lambda way=way: ref_y(p, k, way, 1), beside)

    def need_units(j):
        for p in range(j + 1):
            for k in range(nx):
                need_z(p, k, 0)
                need_y(p, k)
                need_z(p, k, 1)

    def tiles_of(span, fn):
        @pl.loop(0, span // TILE)
        def _(i):
            fn(pl.ds(pl.multiple_of(i * TILE, TILE), TILE))

    def gather_z(p, k, piece):
        need_z(p, k, piece)
        for way in both:
            def make(way=way):
                ref = ref_z(p, k, way, piece)
                return ref, ref
            send(("gz", p, k, way, piece), held(p, way) & open_to(way), make, along(step(way)))

    def gather_y(p, k):
        need_z(p, k, 0)
        for way in both if p else both[:1]:
            send(("gy", p, k, way), held(p, way) if p else None,
                 lambda way=way: (ref_y(p, k, way, 0), ref_y(p, k, way, 1)), beside)

    def sum_y(p, k):
        for way in both[:1] if p == na else both:
            def make(way=way):
                t = target(p, way)
                return psy.at[k, t], ry.at[k, t]
            send(("sy", p, k, way), None if p == na else due(p, way), make, beside)

    def sum_z(name, p, k):
        part_of, out, into, span = (pa, sa, ra, cut) if name == "sa" else (pb, sb, rb, cols - cut)
        for way in both:
            def run(chained, way=way):
                t = target(p, way)
                if name == "sa":
                    arrive(("sy", p, k, way), ry.at[k, t], beside)
                if chained:
                    arrive((name, p - 1, k, way), into.at[way, k, t], along(-step(way)))

                def tile(at):
                    val = part_of[k, t, ..., at]
                    if name == "sa":
                        val += ry[k, t, :, :, at].astype(F32)
                    if chained:
                        val += into[way, k, t, ..., at].astype(F32)
                    out[k, t, ..., at] = val.astype(BF16)

                tiles_of(span, tile)

            now = due(p, way)
            pl.when(now & open_from(way))(lambda: run(True))
            pl.when(now & jnp.logical_not(open_from(way)))(lambda: run(False))

            def make(way=way):
                t = target(p, way)
                return out.at[k, t], into.at[way, k, t]
            send((name, p, k, way), now, make, along(step(way)))

    def add_last(name, k):
        total, into, span = (pa, ra, cut) if name == "sa" else (pb, rb, cols - cut)
        for way in both:
            def run(way=way):
                arrive((name, na - 1, k, way), into.at[way, k, z], along(-step(way)))

                def tile(at):
                    total[k, z, ..., at] += into[way, k, z, ..., at].astype(F32)
                tiles_of(span, tile)
            pl.when(open_from(way))(run)

    def put(kx, kc):
        val = (blocks[kx, kc].astype(F32) * gate[...]).astype(BF16).reshape(na, 2, rows, width)
        for bb in range(2):
            gated[(b + bb) % 2, kx, :, kc] = val[:, bb]

    def passed(k):
        arrive(("attn", k), blocks.at[k, 0], dp(behind((k, 0))))
        send(("pass", k), None, lambda: (blocks.at[k, 0], blocks.at[k, 1]), sibling)
        make_gate()
        put(k, 0)

    def make_gate():
        if "gate" in seen:
            return
        seen.add("gate")
        copied(mask_copy)
        copied(scale_copy)
        heads = scale.shape[0]
        each = width // heads
        for i in range(heads):
            gate[:, i * each:(i + 1) * each] = jnp.full((1, each), mask[i].astype(F32) * scale[i], F32)

    def take(k):
        make_gate()
        if k:
            arrive(("pass", k), blocks.at[k, 1], sibling)
        else:
            copied(attn_copy)
            put(0, 0)
            arrive(("attn", 0), blocks.at[0, 1], sibling)
        put(k, 1)

    def turn(k):
        span = na * 2 * rows
        for r in range(2):
            lo = (r * nx + k) * span
            gt[:, lo:lo + span] = gated[r, k].reshape(span, width).T

    def project(k):
        copied(w_copy)

        def dot(at):
            lhs = gated[:, k].reshape(2 * na * 2 * rows, width)
            res = jnp.dot(lhs, w[:, at], preferred_element_type=F32)
            return res.reshape(2, na, 2, rows, TILE)

        def front(at):
            res = dot(at)
            pa[k, :, :, :, at] = res[0]
            psy[k, :, :, :, at] = res[1].astype(BF16)

        @pl.loop(cut // TILE, cols // TILE)
        def _(i):
            res = dot(pl.ds(pl.multiple_of(i * TILE, TILE), TILE))
            low = pl.ds(pl.multiple_of(i * TILE - cut, TILE), TILE)
            for r in range(2):
                pb[k, :, r, :, :, low] = res[r]

        tiles_of(cut, front)

    small = jnp.minimum(z, na - 1 - z)

    def nth(j):
        if j == 0:
            return z
        near = z - (j + 1) // 2 if j % 2 else z + (j + 1) // 2
        end = jnp.where(z == small, j, na - 1 - j)
        return jnp.where(j <= 2 * small, near, end)

    def back(j):
        need_units(j)
        copied(w_copy)
        u = nth(j)

        def tile(at):
            lhs = g[:, :, u].reshape(2 * nx * 2 * rows, cols)
            res = lax.dot_general(lhs, w[at, :], (((1,), (1,)), ((), ())), preferred_element_type=F32)
            res = res.reshape(2, nx, 2, rows, TILE)
            bs[j, :, :, :, at] = res[:, :, 1].astype(BF16)
            bo[j, :, :, :, at] = res[:, :, 0]

        tiles_of(width, tile)
        send(("pair", j), None, lambda: (bs.at[j], br.at[j]), sibling)

    def cross(j):
        arrive(("pair", j), br.at[j], sibling)
        for k in range(1, nx):
            bs2[j, k - 1] = (bo[j, :, k] + br[j, :, k].astype(F32)).astype(BF16)
            send(("cross", j, k), None, lambda k=k: (bs2.at[j, k - 1], br2.at[j, k - 1]), dp(behind((k, 0))))

    def attn_out(j):
        for k in range(1, nx):
            arrive(("cross", j, k), br2.at[j, k - 1], dp(ahead((k, 0))))
        total = bo[j, :, 0] + br[j, :, 0].astype(F32)
        for k in range(1, nx):
            total += br2[j, k - 1].astype(F32)
        total = (total * gate[...].reshape(1, 1, width)).astype(BF16)
        for r in range(2):
            ga[nth(j), (b + r) % 2] = total[r]
        copy(ga.at[nth(j)], ga_out.at[nth(j)])

    def weight(i):
        need_units(na - 1)
        slot, each = len(tiles) % SLOTS, cols // nd
        if len(tiles) >= SLOTS:
            copied(tiles[-SLOTS])
        at = slice(i * TILE, (i + 1) * TILE)
        gw[slot] = jnp.dot(gt[...], g[:, :, :, :, :, at].reshape(tokens, TILE), preferred_element_type=F32)
        lo = i * TILE % each
        tiles.append(copy(gw.at[slot], gw_outs[i * TILE // each].at[:, lo:lo + TILE]))

    def last_b(k):
        add_last("sb", k)
        fb[k] = pb[k, z, 1].astype(BF16)
        send(("fy", k), None, lambda: (fb.at[k], ryf.at[k]), beside)

    def finish(k):
        arrive(("sy", na, k, RIGHT), ry.at[k, z], beside)

        def tile(at):
            fin[k, :, :, at] = (pa[k, z, :, :, at] + ry[k, z, :, :, at].astype(F32)).astype(BF16)

        tiles_of(cut, tile)
        arrive(("fy", k), ryf.at[k], beside)
        fin[k, :, :, rest] = (pb[k, z, 0] + ryf[k].astype(F32)).astype(BF16)
        for kc in range(2):
            if (k, kc) != (0, 0):
                send(("home", (k, kc)), None, lambda kc=kc: (fin.at[k, kc], pj.at[d]), dp(behind((k, kc))))
            else:
                pj[d] = fin[0, 0]
                copy(pj.at[d], pj_out.at[d])

    steps = {
        "gz": gather_z, "gy": gather_y, "sy": sum_y, "sa": functools.partial(sum_z, "sa"),
        "sb": functools.partial(sum_z, "sb"), "pass": passed, "put": take, "proj": project, "turn": turn,
        "back": back, "cross": cross, "ga": attn_out, "gw": weight, "fb": last_b,
        "fa": functools.partial(add_last, "sa"), "fin": finish,
    }
    for name, *at in plan(na, nx, cols // TILE):
        steps[name](*at)
    for s in [(0, 1)] + far:
        arrive(("home", s), pj.at[ahead(s)], dp(ahead(s)))
        copy(pj.at[ahead(s)], pj_out.at[ahead(s)])
    for key, cond, make, dev in sent:
        when(cond, lambda: remote(key, *make(), dev).wait_send())
    for i in range(len(local)):
        copied(i)


def hand_over(pj, ga, *refs):
    *gw, proj, gattn, gw_out, sems = refs
    cols = pj.shape[2]
    each = cols // len(gw)
    pairs = [(ga, gattn)]
    for i in range(len(gw)):
        pairs.append((gw[i], gw_out.at[:, i * each:(i + 1) * each]))
        pairs.append((pj.at[i], proj.at[:, i * cols:(i + 1) * cols]))
    copies = [pltpu.make_async_copy(src, dst, sems.at[i]) for i, (src, dst) in enumerate(pairs)]
    for copy in copies:
        copy.start()
    for copy in copies:
        copy.wait()


def fused(nh, nd, attn_out, head_mask, gate_scale, w_out, grad_out):
    na, nx = nh // 2, nd // 2
    rows, cols, width = grad_out.shape[0], w_out.shape[1], w_out.shape[0]
    tokens = rows * nh * nd
    cut = split(cols)
    n_sems = 2 * nd + 4 * nx + 11 * (na + 1) * nx * 2 + na * nx
    vmem = pl.BlockSpec(memory_space=pltpu.VMEM)
    hbm = pl.BlockSpec(memory_space=pltpu.HBM)
    free = pl.BlockSpec(memory_space=pl.ANY)
    order = (2, nx, na, 2, rows)
    half = (nx, na, 2, rows)
    whole = (nx, na, 2, 2, rows)
    pj, ga, *gw = pl.pallas_call(
        functools.partial(kernel, nh, nd),
        out_shape=(
            jax.ShapeDtypeStruct((nd, rows, cols), BF16),
            jax.ShapeDtypeStruct((na, 2, rows, width), BF16),
        ) + (jax.ShapeDtypeStruct((width, cols // nd), F32),) * nd,
        in_specs=[hbm] * 5,
        out_specs=(free,) * (2 + nd),
        scratch_shapes=[
            pltpu.SMEM(head_mask.shape, head_mask.dtype),
            pltpu.SMEM(gate_scale.shape, F32),
            pltpu.VMEM((1, width), F32),
            pltpu.VMEM((nx, 2, nh * rows, width), BF16),
            pltpu.VMEM(order + (width,), BF16),
            pltpu.VMEM((width, tokens), BF16),
            pltpu.VMEM(w_out.shape, BF16),
            pltpu.VMEM(order + (cols,), BF16),
            pltpu.VMEM(half + (cut,), F32),
            pltpu.VMEM(whole + (cols - cut,), F32),
            pltpu.VMEM(half + (cut,), BF16),
            pltpu.VMEM(half + (cut,), BF16),
            pltpu.VMEM(half + (cut,), BF16),
            pltpu.VMEM(whole + (cols - cut,), BF16),
            pltpu.VMEM((2,) + half + (cut,), BF16),
            pltpu.VMEM((2,) + whole + (cols - cut,), BF16),
            pltpu.VMEM((nx, 2, rows, cols - cut), BF16),
            pltpu.VMEM((nx, 2, rows, cols - cut), BF16),
            pltpu.VMEM((nx, 2, rows, cols), BF16),
            pltpu.VMEM((nd, rows, cols), BF16),
            pltpu.VMEM((na, 2, nx, rows, width), BF16),
            pltpu.VMEM((na, 2, nx, rows, width), F32),
            pltpu.VMEM((na, 2, nx, rows, width), BF16),
            pltpu.VMEM((na, nx - 1, 2, rows, width), BF16),
            pltpu.VMEM((na, nx - 1, 2, rows, width), BF16),
            pltpu.VMEM((na, 2, rows, width), BF16),
            pltpu.VMEM((SLOTS, width, TILE), F32),
            pltpu.SemaphoreType.DMA((n_sems,)),
            pltpu.SemaphoreType.DMA((n_sems,)),
            pltpu.SemaphoreType.DMA((5 + nd + na + cols // TILE,)),
        ],
        compiler_params=pltpu.CompilerParams(
            collective_id=0, has_side_effects=True, vmem_limit_bytes=VMEM_LIMIT
        ),
    )(*[pltpu.with_memory_space_constraint(a, pltpu.HBM) for a in (attn_out, head_mask, gate_scale, grad_out, w_out)])
    proj, gattn, gw = pl.pallas_call(
        hand_over,
        out_shape=(
            jax.ShapeDtypeStruct(grad_out.shape, BF16),
            jax.ShapeDtypeStruct(attn_out.shape, BF16),
            jax.ShapeDtypeStruct(w_out.shape, F32),
        ),
        in_specs=[vmem] * (2 + nd),
        out_specs=(hbm,) * 3,
        scratch_shapes=[pltpu.SemaphoreType.DMA((2 * nd + 1,))],
        compiler_params=pltpu.CompilerParams(vmem_limit_bytes=HAND_LIMIT),
    )(pj, ga.reshape(attn_out.shape), *gw)
    return proj, gattn, gw


def shards(attn_out, head_mask, gate_scale, w_out, grad_out):
    n_dp, n_head = lax.axis_size("dp"), lax.axis_size("head")
    rows, (width, cols) = grad_out.shape[0], w_out.shape
    if rows % 16 == 0 and n_dp % 2 == 0 and n_head % 2 == 0 and min(n_dp, n_head) > 2 and width % TILE == 0 and cols % (2 * TILE) == 0 and cols % (n_dp * 128) == 0 and (width // head_mask.shape[0]) % 128 == 0:
        return fused(n_head, n_dp, attn_out, head_mask, gate_scale, w_out, grad_out)
    gate_vals = head_mask.astype(jnp.float32) * gate_scale
    width_each = attn_out.shape[1] // gate_vals.shape[0]
    col_gate = jnp.repeat(gate_vals, width_each)
    gated = (attn_out.astype(jnp.float32) * col_gate[None, :]).astype(jnp.bfloat16)
    mine = lax.all_to_all(grad_out, "dp", 1, 0, tiled=True)
    every = lax.all_gather(mine.reshape(n_dp, rows, cols), "head", axis=1)
    grad_cols = every.reshape(n_dp * n_head * rows, cols)
    gated_all = lax.all_gather(gated, "dp", axis=0, tiled=True)
    part = jnp.dot(gated_all, w_out, preferred_element_type=jnp.float32).astype(jnp.bfloat16)
    summed = lax.psum_scatter(part.reshape(n_dp, n_head, rows, cols), "head", scatter_dimension=1, tiled=False)
    proj_out = lax.all_to_all(summed.reshape(n_dp * rows, cols), "dp", 0, 1, tiled=True)
    back = lax.dot_general(grad_cols, w_out, (((1,), (1,)), ((), ())), preferred_element_type=jnp.float32)
    back = lax.psum_scatter(back.astype(jnp.bfloat16), "dp", scatter_dimension=0, tiled=True)
    grad_attn = (back.astype(jnp.float32) * col_gate[None, :]).astype(jnp.bfloat16)
    grad_w = lax.dot_general(gated_all, grad_cols, (((0,), (0,)), ((), ())), preferred_element_type=jnp.float32)
    return (proj_out, grad_attn, grad_w)


def solution(mesh):
    return jax.shard_map(
        shards,
        mesh=mesh,
        in_specs=(P("dp", "head"), P("head"), P("head"), P("head", "dp"), P(("dp", "head"), None)),
        out_specs=(P(("dp", "head"), None), P("dp", "head"), P("head", "dp")),
        check_vma=False,
    )
```

time: 93.4 us -> 83.6 us (0.90); the launches traced: 91.9 us -> 83.4 us
  Pallas kernels: 91.3 us -> 82.8 us
    pallas_call x1, Pallas kernels: 84.8 us -> 79.1 us  [fused(): pl.pallas_call(functools.partial(kernel, nh, nd), out_shape=(jax.ShapeDty...]
    pallas_call x1, Pallas kernels: 6.46 us -> 3.71 us  [fused(): pl.pallas_call(hand_over, out_shape=(jax.ShapeDtypeStruct(grad_out.shape,...]
where the time goes in v3:
time: 83.6 us; the launch traced here: 83.4 us
  Pallas kernels  82.8 us (99%)
    pallas_call x1, Pallas kernels, fused(): pl.pallas_call(functools.partial(kernel, nh, nd), out_shape=(jax.ShapeDty...  79.1 us
    pallas_call x1, Pallas kernels, fused(): pl.pallas_call(hand_over, out_shape=(jax.ShapeDtypeStruct(grad_out.shape,...  3.71 us

profile of v3, /device:TPU:0, one launch (start us, length us, event | category | flops | bytes accessed | tf_op | source)
XLA Modules:
  0.0 83.4 jit_solution(3310857025403757875)
XLA Ops:
  0.6 79.1 %shard_map.76 = (bf16[4,32,2048]{2,1,0:T(8,128)(2,1)S(1)}, bf16[4,2,32,1024]{3,2,1,0:T(8,128)(2,1)S(1)}, f32[1024,512]{1,0:T(8,128)S(1)}, f32[1024,512]{1,0:T(8,...) custom-call(bf16[256,1024]{1,0:T(8,128)(2,1)} %attn.1, s32[8]{0:T(128)} %mask_hbm.1, f32[8]{0:T(128)} %scale_hbm.1, ...), custom_call_target="tpu_custom_call" | custom-call | tf_op jit(solution)/shard_map/pallas_call | solution.py:452
  79.7 3.7 %shard_map.77 = (bf16[32,8192]{1,0:T(8,128)(2,1)}, bf16[256,1024]{1,0:T(8,128)(2,1)}, f32[1024,2048]{1,0:T(8,128)}) custom-call(bf16[4,32,2048]{2,1,0:T(8,128)(2,1)S(1)} %get-tuple-element.9.pj, bf16[256,1024]{1,0:T(8,128)(2,1)S(1)} %bitcast.1, f32[1024,512]{1,0:T(8,128)S(1)} %get-tuple-element.11.refs_0_, f32[1024,512]{1,0:T(8,128)S(1)} %get-tuple-element.12.refs_1_, ...), custom_call_target="tpu_custom_call" | custom-call | tf_op jit(solution)/shard_map/pallas_call | solution.py:496

commit v4 on v3

--- a/solution.py
+++ b/solution.py
@@ -10,35 +10,37 @@
 MESH = pl.DeviceIdType.MESH
 F32, BF16 = jnp.float32, jnp.bfloat16
 TILE = 256
-SHARE = 5, 8
+SUM_SHARE = 5, 8
+GATHER_SHARE = 9, 16
 VMEM_LIMIT = 41 * 1024 * 1024
 HAND_LIMIT = 2 * 1024 * 1024
 SLOTS = 3
 
 
 ORDER = (
-    ("gy", 0, 0), ("gz", 0, 0, 0), ("put", 0), ("proj", 0), ("sy", 2, 0), ("turn", 0), ("sb", 1, 0),
-    ("gy", 0, 1), ("gz", 0, 1, 0), ("gz", 1, 0, 0), ("sy", 1, 0), ("gz", 0, 0, 1), ("gy", 1, 0), ("sb", 2, 0),
-    ("gy", 1, 1), ("pass", 1), ("gz", 0, 1, 1), ("gy", 2, 0), ("gz", 1, 1, 0), ("put", 1), ("gz", 1, 0, 1),
-    ("gz", 2, 0, 0), ("proj", 1), ("sb", 1, 1), ("sb", 2, 1), ("sy", 2, 1), ("gz", 2, 1, 0), ("gz", 1, 1, 1),
-    ("sa", 1, 0), ("back", 1), ("sy", 1, 1), ("gy", 2, 1), ("sa", 1, 1), ("turn", 1), ("sy", 3, 1),
-    ("sb", 3, 1), ("gy", 3, 0), ("cross", 1), ("back", 0), ("sa", 2, 1), ("gy", 3, 1), ("gz", 2, 0, 1),
-    ("back", 2), ("ga", 1), ("sy", 3, 0), ("cross", 2), ("cross", 0), ("gz", 2, 1, 1), ("fb", 1),
-    ("sy", 4, 1), ("sa", 2, 0), ("sa", 3, 1), ("sb", 3, 0), ("back", 3), ("gw", 6), ("sy", 4, 0),
-    ("sa", 3, 0), ("cross", 3), ("gw", 3), ("gw", 4), ("ga", 2), ("fa", 1), ("fin", 1), ("gw", 1), ("fb", 0),
-    ("ga", 0), ("gw", 5), ("gw", 2), ("ga", 3), ("gw", 7), ("fa", 0), ("fin", 0), ("gw", 0),
+    ("oy", 0, 1), ("oz", 0, 1), ("put", 0), ("oy", 1, 0), ("oz", 1, 0), ("oz", 1, 1), ("oy", 1, 1),
+    ("gy", 1, 0), ("gz", 0, 0, 1), ("proj", 0), ("gz", 1, 0, 0), ("sy", 1, 0), ("turn", 0), ("sb", 1, 0),
+    ("gz", 0, 1, 1), ("back", 0), ("gy", 1, 1), ("gz", 1, 1, 0), ("sy", 2, 0), ("sb", 2, 0), ("pass", 1),
+    ("sa", 1, 0), ("put", 1), ("gz", 2, 0, 0), ("gy", 2, 0), ("proj", 1), ("sy", 1, 1), ("gz", 1, 1, 1),
+    ("sy", 2, 1), ("sb", 1, 1), ("back", 1), ("sa", 1, 1), ("gy", 2, 1), ("gz", 1, 0, 1), ("cross", 1),
+    ("gy", 3, 0), ("sb", 2, 1), ("cross", 0), ("gz", 2, 1, 0), ("sy", 3, 1), ("gz", 2, 1, 1), ("sa", 2, 1),
+    ("sa", 2, 0), ("gz", 2, 0, 1), ("ga", 1), ("back", 2), ("gy", 3, 1), ("sy", 3, 0), ("sb", 3, 1),
+    ("cross", 2), ("turn", 1), ("ga", 0), ("sy", 4, 1), ("sa", 3, 1), ("sb", 3, 0), ("back", 3), ("gw", 7),
+    ("ga", 2), ("fb", 1), ("cross", 3), ("gw", 6), ("sa", 3, 0), ("sy", 4, 0), ("gw", 5), ("fa", 1),
+    ("fin", 1), ("gw", 3), ("ga", 3), ("fb", 0), ("gw", 0), ("gw", 1), ("gw", 4), ("fa", 0), ("fin", 0),
+    ("gw", 2),
 )
 
 
-def split(cols):
-    tiles = cols // TILE
-    return max(1, min(tiles - 1, tiles * SHARE[0] // SHARE[1])) * TILE
+def split(cols, share, tile):
+    tiles = cols // tile
+    return max(1, min(tiles - 1, tiles * share[0] // share[1])) * tile
 
 
 def plan(na, nx, tiles):
-    order = [("gz", 0, 0, 0), ("gy", 0, 0), ("put", 0), ("proj", 0)]
+    order = [("oz", 0, 1), ("oy", 0, 1), ("put", 0), ("proj", 0)]
     for k in range(1, nx):
-        order += [("gz", 0, k, 0), ("gy", 0, k)]
+        order += [(name, k, kc) for kc in range(2) for name in ("oz", "oy")]
     order += [("gz", 0, 0, 1), ("sy", 1, 0), ("turn", 0)]
     for k in range(1, nx):
         order += [("gz", 0, k, 1), ("pass", k)]
@@ -59,6 +61,12 @@
     return ORDER if set(ORDER) == set(order) else order
 
 
+def semaphores(na, nx, tiles):
+    each = {"oz": 2, "oy": 1, "gz": 2, "gy": 2, "sy": 2, "sa": 2, "sb": 2, "pass": 1, "back": 1,
+            "cross": nx - 1, "fb": 1, "fin": 2}
+    return 3 + 2 * nx + nx + sum(each.get(step[0], 0) for step in plan(na, nx, tiles))
+
+
 def kernel(nh, nd, attn, mask_hbm, scale_hbm, grad, w_hbm, pj_out, ga_out, *more):
     gw_outs, more = more[:nd], more[nd:]
     (mask, scale, gate, blocks, gated, gt, w, g, pa, pb, psy, ry, sa, sb, ra, rb, fb, ryf, fin, pj,
@@ -69,8 +77,8 @@
     x, c = d // 2, d % 2
     rows, cols = g.shape[-2:]
     width, tokens = gt.shape
-    cut = split(cols)
-    first, rest = pl.ds(0, cut), pl.ds(cut, cols - cut)
+    cut, mid = split(cols, SUM_SHARE, TILE), split(cols, GATHER_SHARE, 128)
+    first, rest = pl.ds(0, mid), pl.ds(mid, cols - mid)
     sent, ids, seen = [], {}, set()
     local, tiles = [], []
 
@@ -81,9 +89,11 @@
             pl.when(cond)(fn)
 
     def remote(key, src, dst, dev):
+        if key[0] in ("gz", "sa", "sb"):
+            key = ("z", *key[1:4], key[4] if key[0] == "gz" else int(key[0] == "sb"))
         i = ids.setdefault(key, len(ids))
         return pltpu.make_async_remote_copy(
-            src_ref=src, dst_ref=dst, send_sem=ssem.at[i], recv_sem=rsem.at[i],
+            src_ref=src, dst_ref=dst, send_sem=ssem.at[0], recv_sem=rsem.at[i],
             device_id=dev, device_id_type=MESH,
         )
 
@@ -147,28 +157,45 @@
     pl.when(z < na - 1)(lambda: greet(along(1)))
     pl.semaphore_wait(barrier, nd + (z + na - 1) // na + (2 * na - 2 - z) // na)
 
+    both = RIGHT, LEFT = 0, 1
+
+    def open_to(way):
+        return z < na - 1 if way == RIGHT else z > 0
+
+    def open_from(way):
+        return z > 0 if way == RIGHT else z < na - 1
+
+    def step(way):
+        return 1 if way == RIGHT else -1
+
+    def offer_z(k, kc):
+        need_own(k, kc)
+        src = g.at[0, k, z, kc] if k or kc else part(d)
+        for way in both:
+            send(("oz", k, kc, way), open_to(way), lambda: (src, g.at[0, k, z, kc]), along(step(way)))
+
+    def offer_y(k, kc):
+        need_own(k, kc)
+        src = g.at[0, k, z, kc] if k or kc else part(d)
+        send(("oy", k, kc), None, lambda: (src, g.at[1, k, z, kc]), beside)
+
+    def need_own(k, kc):
+        if k or kc:
+            once(("swap", (k, kc)), None, lambda: g.at[0, k, z, kc], dp(behind((k, kc))))
+
+    offer_z(0, 0)
+    offer_y(0, 0)
     for s in far + [(0, 1)]:
         send(("swap", s), None, lambda s=s: (part(ahead(s)), g.at[0, s[0], z, s[1]]), dp(ahead(s)))
     for k in range(1, nx):
         send(("attn", k), None, lambda k=k: (attn, blocks.at[k, 0]), dp(ahead((k, 0))))
     send(("attn", 0), None, lambda: (attn, blocks.at[0, 1]), sibling)
 
-    both = RIGHT, LEFT = 0, 1
-
     def unit(p, way):
         return z - p if way == RIGHT else z + p
 
     def held(p, way):
         return z >= p if way == RIGHT else z + p <= na - 1
-
-    def open_to(way):
-        return z < na - 1 if way == RIGHT else z > 0
-
-    def open_from(way):
-        return z > 0 if way == RIGHT else z < na - 1
-
-    def step(way):
-        return 1 if way == RIGHT else -1
 
     def due(p, way):
         return p > z if way == RIGHT else p > na - 1 - z
@@ -181,24 +208,29 @@
         return g.at[0, k, u] if piece == 0 else g.at[1, k, u, :, :, rest]
 
     def ref_y(p, k, way, r):
-        return g.at[r, k, z] if p == 0 else g.at[r, k, unit(p, way), :, :, first]
+        return g.at[r, k, unit(p, way), :, :, first]
 
     def need_z(p, k, piece):
-        if p:
-            for way in both:
-                once(("gz", p - 1, k, way, piece), held(p, way), lambda way=way: ref_z(p, k, way, piece), along(-step(way)))
-        elif piece:
+        if p == 0 and piece:
             need_y(0, k)
-        else:
-            for s in ((k, 0), (k, 1)):
-                if s == (0, 0):
-                    copied(own_copy)
-                else:
-                    once(("swap", s), None, lambda s=s: g.at[0, s[0], z, s[1]], dp(behind(s)))
+        elif p == 0:
+            if k == 0:
+                copied(own_copy)
+            need_own(k, 0)
+            need_own(k, 1)
+        for way in both if p else ():
+            if p == 1 and piece == 0:
+                for kc in range(2):
+                    once(("oz", k, kc, way), held(p, way), lambda: g.at[0, k, unit(p, way), kc], along(-step(way)))
+            else:
+                once(("gz", p - 1, k, way, piece), held(p, way), lambda: ref_z(p, k, way, piece), along(-step(way)))
 
     def need_y(p, k):
-        for way in both if p else both[:1]:
-            once(("gy", p, k, way), held(p, way) if p else None, lambda way=way: ref_y(p, k, way, 1), beside)
+        if p == 0:
+            for kc in range(2):
+                once(("oy", k, kc), None, lambda: g.at[1, k, z, kc], beside)
+        for way in both if p else ():
+            once(("gy", p, k, way), held(p, way), lambda: ref_y(p, k, way, 1), beside)
 
     def need_units(j):
         for p in range(j + 1):
@@ -222,8 +254,8 @@
 
     def gather_y(p, k):
         need_z(p, k, 0)
-        for way in both if p else both[:1]:
-            send(("gy", p, k, way), held(p, way) if p else None,
+        for way in both:
+            send(("gy", p, k, way), held(p, way),
                  lambda way=way: (ref_y(p, k, way, 0), ref_y(p, k, way, 1)), beside)
 
     def sum_y(p, k):
@@ -397,7 +429,7 @@
 
         tiles_of(cut, tile)
         arrive(("fy", k), ryf.at[k], beside)
-        fin[k, :, :, rest] = (pb[k, z, 0] + ryf[k].astype(F32)).astype(BF16)
+        fin[k, :, :, cut:] = (pb[k, z, 0] + ryf[k].astype(F32)).astype(BF16)
         for kc in range(2):
             if (k, kc) != (0, 0):
                 send(("home", (k, kc)), None, lambda kc=kc: (fin.at[k, kc], pj.at[d]), dp(behind((k, kc))))
@@ -406,7 +438,7 @@
                 copy(pj.at[d], pj_out.at[d])
 
     steps = {
-        "gz": gather_z, "gy": gather_y, "sy": sum_y, "sa": functools.partial(sum_z, "sa"),
+        "oz": offer_z, "oy": offer_y, "gz": gather_z, "gy": gather_y, "sy": sum_y, "sa": functools.partial(sum_z, "sa"),
         "sb": functools.partial(sum_z, "sb"), "pass": passed, "put": take, "proj": project, "turn": turn,
         "back": back, "cross": cross, "ga": attn_out, "gw": weight, "fb": last_b,
         "fa": functools.partial(add_last, "sa"), "fin": finish,
@@ -441,8 +473,8 @@
     na, nx = nh // 2, nd // 2
     rows, cols, width = grad_out.shape[0], w_out.shape[1], w_out.shape[0]
     tokens = rows * nh * nd
-    cut = split(cols)
-    n_sems = 2 * nd + 4 * nx + 11 * (na + 1) * nx * 2 + na * nx
+    cut = split(cols, SUM_SHARE, TILE)
+    n_sems = semaphores(na, nx, cols // TILE)
     vmem = pl.BlockSpec(memory_space=pltpu.VMEM)
     hbm = pl.BlockSpec(memory_space=pltpu.HBM)
     free = pl.BlockSpec(memory_space=pl.ANY)
@@ -485,7 +517,7 @@
             pltpu.VMEM((na, nx - 1, 2, rows, width), BF16),
             pltpu.VMEM((na, 2, rows, width), BF16),
             pltpu.VMEM((SLOTS, width, TILE), F32),
-            pltpu.SemaphoreType.DMA((n_sems,)),
+            pltpu.SemaphoreType.DMA((1,)),
             pltpu.SemaphoreType.DMA((n_sems,)),
             pltpu.SemaphoreType.DMA((5 + nd + na + cols // TILE,)),
         ],

time: 83.6 us -> 79 us (0.945)
  Pallas kernels: 82.8 us -> 78.2 us
    pallas_call x1, Pallas kernels: 79.1 us -> 74.5 us  [fused(): pl.pallas_call(functools.partial(kernel, nh, nd), out_shape=(jax.ShapeDty...]
where the time goes in v4:
time: 79 us; the launch traced here: 78.8 us
  Pallas kernels  78.2 us (99%)
    pallas_call x1, Pallas kernels, fused(): pl.pallas_call(functools.partial(kernel, nh, nd), out_shape=(jax.ShapeDty...  74.5 us
    pallas_call x1, Pallas kernels, fused(): pl.pallas_call(hand_over, out_shape=(jax.ShapeDtypeStruct(grad_out.shape,...  3.71 us

profile of v4, /device:TPU:0, one launch (start us, length us, event | category | flops | bytes accessed | tf_op | source)
XLA Modules:
  0.0 78.8 jit_solution(13168287605780768047)
XLA Ops:
  0.6 74.5 %shard_map.76 = (bf16[4,32,2048]{2,1,0:T(8,128)(2,1)S(1)}, bf16[4,2,32,1024]{3,2,1,0:T(8,128)(2,1)S(1)}, f32[1024,512]{1,0:T(8,128)S(1)}, f32[1024,512]{1,0:T(8,...) custom-call(bf16[256,1024]{1,0:T(8,128)(2,1)} %attn.1, s32[8]{0:T(128)} %mask_hbm.1, f32[8]{0:T(128)} %scale_hbm.1, ...), custom_call_target="tpu_custom_call" | custom-call | tf_op jit(solution)/shard_map/pallas_call | solution.py:484
  75.1 3.7 %shard_map.77 = (bf16[32,8192]{1,0:T(8,128)(2,1)}, bf16[256,1024]{1,0:T(8,128)(2,1)}, f32[1024,2048]{1,0:T(8,128)}) custom-call(bf16[4,32,2048]{2,1,0:T(8,128)(2,1)S(1)} %get-tuple-element.9.pj, bf16[256,1024]{1,0:T(8,128)(2,1)S(1)} %bitcast.1, f32[1024,512]{1,0:T(8,128)S(1)} %get-tuple-element.11.refs_0_, f32[1024,512]{1,0:T(8,128)S(1)} %get-tuple-element.12.refs_1_, ...), custom_call_target="tpu_custom_call" | custom-call | tf_op jit(solution)/shard_map/pallas_call | solution.py:528

commit v5 on v4

--- a/solution.py
+++ b/solution.py
@@ -18,17 +18,17 @@
 
 
 ORDER = (
-    ("oy", 0, 1), ("oz", 0, 1), ("put", 0), ("oy", 1, 0), ("oz", 1, 0), ("oz", 1, 1), ("oy", 1, 1),
-    ("gy", 1, 0), ("gz", 0, 0, 1), ("proj", 0), ("gz", 1, 0, 0), ("sy", 1, 0), ("turn", 0), ("sb", 1, 0),
-    ("gz", 0, 1, 1), ("back", 0), ("gy", 1, 1), ("gz", 1, 1, 0), ("sy", 2, 0), ("sb", 2, 0), ("pass", 1),
-    ("sa", 1, 0), ("put", 1), ("gz", 2, 0, 0), ("gy", 2, 0), ("proj", 1), ("sy", 1, 1), ("gz", 1, 1, 1),
-    ("sy", 2, 1), ("sb", 1, 1), ("back", 1), ("sa", 1, 1), ("gy", 2, 1), ("gz", 1, 0, 1), ("cross", 1),
-    ("gy", 3, 0), ("sb", 2, 1), ("cross", 0), ("gz", 2, 1, 0), ("sy", 3, 1), ("gz", 2, 1, 1), ("sa", 2, 1),
-    ("sa", 2, 0), ("gz", 2, 0, 1), ("ga", 1), ("back", 2), ("gy", 3, 1), ("sy", 3, 0), ("sb", 3, 1),
-    ("cross", 2), ("turn", 1), ("ga", 0), ("sy", 4, 1), ("sa", 3, 1), ("sb", 3, 0), ("back", 3), ("gw", 7),
-    ("ga", 2), ("fb", 1), ("cross", 3), ("gw", 6), ("sa", 3, 0), ("sy", 4, 0), ("gw", 5), ("fa", 1),
-    ("fin", 1), ("gw", 3), ("ga", 3), ("fb", 0), ("gw", 0), ("gw", 1), ("gw", 4), ("fa", 0), ("fin", 0),
-    ("gw", 2),
+    ("oy", 0, 1), ("oz", 0, 1), ("put", 0), ("oy", 1, 0), ("turn", 0), ("oz", 1, 0), ("oy", 1, 1),
+    ("oz", 1, 1), ("gz", 0, 0, 1), ("proj", 0), ("gz", 1, 0, 0), ("sy", 1, 0), ("sy", 2, 0), ("gz", 0, 1, 1),
+    ("gz", 1, 1, 0), ("gy", 1, 0), ("back", 0), ("sb", 1, 0), ("gy", 1, 1), ("pass", 1), ("sa", 1, 0),
+    ("sb", 2, 0), ("put", 1), ("gz", 2, 0, 0), ("gz", 1, 0, 1), ("proj", 1), ("gz", 1, 1, 1), ("sy", 1, 1),
+    ("sy", 2, 1), ("gy", 2, 0), ("sb", 1, 1), ("cross", 0), ("gz", 2, 1, 0), ("gy", 2, 1), ("turn", 1),
+    ("sa", 1, 1), ("sb", 2, 1), ("sy", 3, 1), ("sa", 2, 1), ("gy", 3, 0), ("gz", 2, 0, 1), ("sa", 2, 0),
+    ("gz", 2, 1, 1), ("back", 2), ("sb", 3, 1), ("gy", 3, 1), ("sy", 3, 0), ("cross", 2), ("back", 1),
+    ("ga", 0), ("sy", 4, 1), ("cross", 1), ("sa", 3, 1), ("back", 3), ("gw", 7), ("sb", 3, 0), ("cross", 3),
+    ("fb", 1), ("gw", 3), ("gw", 5), ("sy", 4, 0), ("gw", 6), ("fa", 1), ("gw", 2), ("fin", 1), ("sa", 3, 0),
+    ("gw", 0), ("fb", 0), ("sc", 3, 0), ("ga", 1), ("gw", 1), ("ga", 2), ("fa", 0), ("gw", 4), ("fin", 0),
+    ("fc", 0), ("ga", 3), ("fic", 0),
 )
 
 
@@ -52,24 +52,24 @@
             order += [("gy", p, k), ("sb", p, k)]
             order += [("gz", p, k, 1)] if p < na - 1 else []
             order += [("sa", p, k), ("sy", p + 1, k)]
+        order += [("sc", p, 0)] if p == na - 1 else []
         order += [("cross", p - 2)] if p > 1 else []
         order += [("back", p - 1)]
     order += [("cross", na - 2), ("back", na - 1)]
     order += [("fb", k) for k in range(nx)] + [("fa", k) for k in range(nx)] + [("cross", na - 1)]
-    order += [("fin", k) for k in reversed(range(nx))]
+    order += [("fin", k) for k in reversed(range(nx))] + [("fc", 0), ("fic", 0)]
     order += [("gw", i) for i in range(tiles)] + [("ga", j) for j in range(na)]
     return ORDER if set(ORDER) == set(order) else order
 
 
 def semaphores(na, nx, tiles):
-    each = {"oz": 2, "oy": 1, "gz": 2, "gy": 2, "sy": 2, "sa": 2, "sb": 2, "pass": 1, "back": 1,
-            "cross": nx - 1, "fb": 1, "fin": 2}
-    return 3 + 2 * nx + nx + sum(each.get(step[0], 0) for step in plan(na, nx, tiles))
+    each = {"oz": 2, "oy": 1, "sy": 2, "sa": 2, "sb": 2, "sc": 2, "pass": 1, "back": 1, "cross": nx - 1, "fb": 1, "fin": 2}
+    return 3 + 2 * nx + nx + 2 * nx + sum(each.get(step[0], 0) for step in plan(na, nx, tiles))
 
 
 def kernel(nh, nd, attn, mask_hbm, scale_hbm, grad, w_hbm, pj_out, ga_out, *more):
     gw_outs, more = more[:nd], more[nd:]
-    (mask, scale, gate, blocks, gated, gt, w, g, pa, pb, psy, ry, sa, sb, ra, rb, fb, ryf, fin, pj,
+    (mask, scale, gate, blocks, gated, gt, w, g, pa, pb, psy, ry, sa, sb, ra, rb, fb, ryf, fin,
      bs, bo, br, bs2, br2, ga, gw, ssem, rsem, lsem) = more
     na, nx = nh // 2, nd // 2
     h, d = lax.axis_index("head"), lax.axis_index("dp")
@@ -91,6 +91,8 @@
     def remote(key, src, dst, dev):
         if key[0] in ("gz", "sa", "sb"):
             key = ("z", *key[1:4], key[4] if key[0] == "gz" else int(key[0] == "sb"))
+        if key[0] in ("gy", "sy"):
+            key = ("y", *key[1:])
         i = ids.setdefault(key, len(ids))
         return pltpu.make_async_remote_copy(
             src_ref=src, dst_ref=dst, send_sem=ssem.at[0], recv_sem=rsem.at[i],
@@ -265,23 +267,34 @@
                 return psy.at[k, t], ry.at[k, t]
             send(("sy", p, k, way), None if p == na else due(p, way), make, beside)
 
+    def half(name, p, k):
+        if (p, k) == (na - 1, 0) and name != "sb":
+            return (1,) if name == "sa" else (0,)
+        return ()
+
     def sum_z(name, p, k):
-        part_of, out, into, span = (pa, sa, ra, cut) if name == "sa" else (pb, sb, rb, cols - cut)
+        rear = name == "sb"
+        total, out, into, span = (pb, sb, rb, cols - cut) if rear else (pa, sa, ra, cut)
+        before = "sb" if rear else "sa"
+        sel = half(name, p, k)
+        fresh = (before, p, k) not in seen
+        seen.add((before, p, k))
         for way in both:
             def run(chained, way=way):
                 t = target(p, way)
-                if name == "sa":
+                if not rear and fresh:
                     arrive(("sy", p, k, way), ry.at[k, t], beside)
-                if chained:
-                    arrive((name, p - 1, k, way), into.at[way, k, t], along(-step(way)))
+                if chained and fresh:
+                    arrive((before, p - 1, k, way), into.at[way, k, t], along(-step(way)))
 
                 def tile(at):
-                    val = part_of[k, t, ..., at]
-                    if name == "sa":
-                        val += ry[k, t, :, :, at].astype(F32)
+                    at = sel + (..., at)
+                    val = total[(k, t) + at]
+                    if not rear:
+                        val += ry[(k, t) + at].astype(F32)
                     if chained:
-                        val += into[way, k, t, ..., at].astype(F32)
-                    out[k, t, ..., at] = val.astype(BF16)
+                        val += into[(way, k, t) + at].astype(F32)
+                    out[(k, t) + at] = val.astype(BF16)
 
                 tiles_of(span, tile)
 
@@ -290,18 +303,20 @@
             pl.when(now & jnp.logical_not(open_from(way)))(lambda: run(False))
 
             def make(way=way):
-                t = target(p, way)
-                return out.at[k, t], into.at[way, k, t]
+                at = (k, target(p, way)) + sel
+                return out.at[at], into.at[(way,) + at]
             send((name, p, k, way), now, make, along(step(way)))
 
     def add_last(name, k):
-        total, into, span = (pa, ra, cut) if name == "sa" else (pb, rb, cols - cut)
+        total, into, span = (pb, rb, cols - cut) if name == "sb" else (pa, ra, cut)
+        sel = half(name, na - 1, k)
         for way in both:
             def run(way=way):
-                arrive((name, na - 1, k, way), into.at[way, k, z], along(-step(way)))
+                arrive((name, na - 1, k, way), into.at[(way, k, z) + sel], along(-step(way)))
 
                 def tile(at):
-                    total[k, z, ..., at] += into[way, k, z, ..., at].astype(F32)
+                    at = sel + (..., at)
+                    total[(k, z) + at] += into[(way, k, z) + at].astype(F32)
                 tiles_of(span, tile)
             pl.when(open_from(way))(run)
 
@@ -421,33 +436,34 @@
         fb[k] = pb[k, z, 1].astype(BF16)
         send(("fy", k), None, lambda: (fb.at[k], ryf.at[k]), beside)
 
-    def finish(k):
-        arrive(("sy", na, k, RIGHT), ry.at[k, z], beside)
+    def finish(k, which):
+        once(("sy", na, k, RIGHT), None, lambda: ry.at[k, z], beside)
 
         def tile(at):
-            fin[k, :, :, at] = (pa[k, z, :, :, at] + ry[k, z, :, :, at].astype(F32)).astype(BF16)
+            for kc in which:
+                fin[k, kc, :, at] = (pa[k, z, kc, :, at] + ry[k, z, kc, :, at].astype(F32)).astype(BF16)
 
         tiles_of(cut, tile)
-        arrive(("fy", k), ryf.at[k], beside)
-        fin[k, :, :, cut:] = (pb[k, z, 0] + ryf[k].astype(F32)).astype(BF16)
-        for kc in range(2):
+        once(("fy", k), None, lambda: ryf.at[k], beside)
+        for kc in which:
+            fin[k, kc, :, cut:] = (pb[k, z, 0, kc] + ryf[k, kc].astype(F32)).astype(BF16)
             if (k, kc) != (0, 0):
-                send(("home", (k, kc)), None, lambda kc=kc: (fin.at[k, kc], pj.at[d]), dp(behind((k, kc))))
+                send(("home", (k, kc)), None, lambda kc=kc: (fin.at[k, kc], pj_out.at[d]), dp(behind((k, kc))))
             else:
-                pj[d] = fin[0, 0]
-                copy(pj.at[d], pj_out.at[d])
+                copy(fin.at[0, 0], pj_out.at[d])
 
     steps = {
         "oz": offer_z, "oy": offer_y, "gz": gather_z, "gy": gather_y, "sy": sum_y, "sa": functools.partial(sum_z, "sa"),
-        "sb": functools.partial(sum_z, "sb"), "pass": passed, "put": take, "proj": project, "turn": turn,
+        "sb": functools.partial(sum_z, "sb"), "sc": functools.partial(sum_z, "sc"), "pass": passed, "put": take, "proj": project, "turn": turn,
         "back": back, "cross": cross, "ga": attn_out, "gw": weight, "fb": last_b,
-        "fa": functools.partial(add_last, "sa"), "fin": finish,
+        "fa": functools.partial(add_last, "sa"), "fc": functools.partial(add_last, "sc"),
+        "fin": lambda k: finish(k, (0, 1) if k else (1,)), "fic": lambda k: finish(k, (0,)),
     }
     for name, *at in plan(na, nx, cols // TILE):
         steps[name](*at)
+    assert len(ids) <= rsem.shape[0]
     for s in [(0, 1)] + far:
-        arrive(("home", s), pj.at[ahead(s)], dp(ahead(s)))
-        copy(pj.at[ahead(s)], pj_out.at[ahead(s)])
+        arrive(("home", s), pj_out.at[ahead(s)], dp(ahead(s)))
     for key, cond, make, dev in sent:
         when(cond, lambda: remote(key, *make(), dev).wait_send())
     for i in range(len(local)):
@@ -458,10 +474,9 @@
     *gw, proj, gattn, gw_out, sems = refs
     cols = pj.shape[2]
     each = cols // len(gw)
-    pairs = [(ga, gattn)]
-    for i in range(len(gw)):
-        pairs.append((gw[i], gw_out.at[:, i * each:(i + 1) * each]))
-        pairs.append((pj.at[i], proj.at[:, i * cols:(i + 1) * cols]))
+    pairs = [(gw[i], gw_out.at[:, i * each:(i + 1) * each]) for i in range(len(gw))]
+    pairs += [(pj.at[i], proj.at[:, i * cols:(i + 1) * cols]) for i in range(len(gw))]
+    pairs.append((ga, gattn))
     copies = [pltpu.make_async_copy(src, dst, sems.at[i]) for i, (src, dst) in enumerate(pairs)]
     for copy in copies:
         copy.start()
@@ -509,7 +524,6 @@
             pltpu.VMEM((nx, 2, rows, cols - cut), BF16),
             pltpu.VMEM((nx, 2, rows, cols - cut), BF16),
             pltpu.VMEM((nx, 2, rows, cols), BF16),
-            pltpu.VMEM((nd, rows, cols), BF16),
             pltpu.VMEM((na, 2, nx, rows, width), BF16),
             pltpu.VMEM((na, 2, nx, rows, width), F32),
             pltpu.VMEM((na, 2, nx, rows, width), BF16),
@@ -519,7 +533,7 @@
             pltpu.VMEM((SLOTS, width, TILE), F32),
             pltpu.SemaphoreType.DMA((1,)),
             pltpu.SemaphoreType.DMA((n_sems,)),
-            pltpu.SemaphoreType.DMA((5 + nd + na + cols // TILE,)),
+            pltpu.SemaphoreType.DMA((6 + na + cols // TILE,)),
         ],
         compiler_params=pltpu.CompilerParams(
             collective_id=0, has_side_effects=True, vmem_limit_bytes=VMEM_LIMIT

time: 79 us -> 77.2 us (0.977)
  Pallas kernels: 78.2 us -> 76.4 us
    pallas_call x1, Pallas kernels: 74.5 us -> 72.8 us  [fused(): pl.pallas_call(functools.partial(kernel, nh, nd), out_shape=(jax.ShapeDty...]
where the time goes in v5:
time: 77.2 us; the launch traced here: 77.1 us
  Pallas kernels  76.4 us (99%)
    pallas_call x1, Pallas kernels, fused(): pl.pallas_call(functools.partial(kernel, nh, nd), out_shape=(jax.ShapeDty...  72.8 us
    pallas_call x1, Pallas kernels, fused(): pl.pallas_call(hand_over, out_shape=(jax.ShapeDtypeStruct(grad_out.shape,...  3.67 us

profile of v5, /device:TPU:0, one launch (start us, length us, event | category | flops | bytes accessed | tf_op | source)
XLA Modules:
  0.0 77.1 jit_solution(8835454799440089056)
XLA Ops:
  0.6 72.8 %shard_map.76 = (bf16[4,32,2048]{2,1,0:T(8,128)(2,1)S(1)}, bf16[4,2,32,1024]{3,2,1,0:T(8,128)(2,1)S(1)}, f32[1024,512]{1,0:T(8,128)S(1)}, f32[1024,512]{1,0:T(8,...) custom-call(bf16[256,1024]{1,0:T(8,128)(2,1)} %attn.1, s32[8]{0:T(128)} %mask_hbm.1, f32[8]{0:T(128)} %scale_hbm.1, ...), custom_call_target="tpu_custom_call" | custom-call | tf_op jit(solution)/shard_map/pallas_call | solution.py:499
  73.4 3.7 %shard_map.77 = (bf16[32,8192]{1,0:T(8,128)(2,1)}, bf16[256,1024]{1,0:T(8,128)(2,1)}, f32[1024,2048]{1,0:T(8,128)}) custom-call(bf16[4,32,2048]{2,1,0:T(8,128)(2,1)S(1)} %get-tuple-element.9.pj, bf16[256,1024]{1,0:T(8,128)(2,1)S(1)} %bitcast.1, f32[1024,512]{1,0:T(8,128)S(1)} %get-tuple-element.11.refs_0_, f32[1024,512]{1,0:T(8,128)S(1)} %get-tuple-element.12.refs_1_, ...), custom_call_target="tpu_custom_call" | custom-call | tf_op jit(solution)/shard_map/pallas_call | solution.py:542

commit v6 on v5

--- a/solution.py
+++ b/solution.py
@@ -172,13 +172,17 @@
 
     def offer_z(k, kc):
         need_own(k, kc)
-        src = g.at[0, k, z, kc] if k or kc else part(d)
+        if (k, kc) == (0, 0):
+            copied(own_copy)
+        src = g.at[0, k, z, kc]
         for way in both:
             send(("oz", k, kc, way), open_to(way), lambda: (src, g.at[0, k, z, kc]), along(step(way)))
 
     def offer_y(k, kc):
         need_own(k, kc)
-        src = g.at[0, k, z, kc] if k or kc else part(d)
+        if (k, kc) == (0, 0):
+            copied(own_copy)
+        src = g.at[0, k, z, kc]
         send(("oy", k, kc), None, lambda: (src, g.at[1, k, z, kc]), beside)
 
     def need_own(k, kc):

time: 77.2 us -> 77 us (level)
  no operation moved by 1% of the time
where the time goes in v6:
time: 77 us; the launch traced here: 76.8 us
  Pallas kernels  76.2 us (99%)
    pallas_call x1, Pallas kernels, fused(): pl.pallas_call(functools.partial(kernel, nh, nd), out_shape=(jax.ShapeDty...  72.5 us
    pallas_call x1, Pallas kernels, fused(): pl.pallas_call(hand_over, out_shape=(jax.ShapeDtypeStruct(grad_out.shape,...  3.67 us

profile of v6, /device:TPU:0, one launch (start us, length us, event | category | flops | bytes accessed | tf_op | source)
XLA Modules:
  0.0 76.8 jit_solution(18241847670109053267)
XLA Ops:
  0.6 72.5 %shard_map.76 = (bf16[4,32,2048]{2,1,0:T(8,128)(2,1)S(1)}, bf16[4,2,32,1024]{3,2,1,0:T(8,128)(2,1)S(1)}, f32[1024,512]{1,0:T(8,128)S(1)}, f32[1024,512]{1,0:T(8,...) custom-call(bf16[256,1024]{1,0:T(8,128)(2,1)} %attn.1, s32[8]{0:T(128)} %mask_hbm.1, f32[8]{0:T(128)} %scale_hbm.1, ...), custom_call_target="tpu_custom_call" | custom-call | tf_op jit(solution)/shard_map/pallas_call | solution.py:503
  73.2 3.7 %shard_map.77 = (bf16[32,8192]{1,0:T(8,128)(2,1)}, bf16[256,1024]{1,0:T(8,128)(2,1)}, f32[1024,2048]{1,0:T(8,128)}) custom-call(bf16[4,32,2048]{2,1,0:T(8,128)(2,1)S(1)} %get-tuple-element.9.pj, bf16[256,1024]{1,0:T(8,128)(2,1)S(1)} %bitcast.1, f32[1024,512]{1,0:T(8,128)S(1)} %get-tuple-element.11.refs_0_, f32[1024,512]{1,0:T(8,128)S(1)} %get-tuple-element.12.refs_1_, ...), custom_call_target="tpu_custom_call" | custom-call | tf_op jit(solution)/shard_map/pallas_call | solution.py:546

commit v7 on v6

--- a/solution.py
+++ b/solution.py
@@ -63,8 +63,8 @@
 
 
 def semaphores(na, nx, tiles):
-    each = {"oz": 2, "oy": 1, "sy": 2, "sa": 2, "sb": 2, "sc": 2, "pass": 1, "back": 1, "cross": nx - 1, "fb": 1, "fin": 2}
-    return 3 + 2 * nx + nx + 2 * nx + sum(each.get(step[0], 0) for step in plan(na, nx, tiles))
+    each = {"sy": 2, "sa": 2, "sb": 2, "sc": 2, "pass": 1, "back": 1, "cross": nx - 1, "fb": 1, "fin": 2}
+    return 8 * nx + sum(each.get(step[0], 0) for step in plan(na, nx, tiles))
 
 
 def kernel(nh, nd, attn, mask_hbm, scale_hbm, grad, w_hbm, pj_out, ga_out, *more):
@@ -93,6 +93,8 @@
             key = ("z", *key[1:4], key[4] if key[0] == "gz" else int(key[0] == "sb"))
         if key[0] in ("gy", "sy"):
             key = ("y", *key[1:])
+        if key[0] in ("oz", "oy"):
+            key = (*key[:2], *key[3:])
         i = ids.setdefault(key, len(ids))
         return pltpu.make_async_remote_copy(
             src_ref=src, dst_ref=dst, send_sem=ssem.at[0], recv_sem=rsem.at[i],
@@ -111,8 +113,8 @@
             seen.add(key)
             when(cond, lambda: arrive(key, make(), dev))
 
-    def copy(src, dst):
-        made = pltpu.make_async_copy(src, dst, lsem.at[len(local)])
+    def copy(src, dst, sem=None):
+        made = pltpu.make_async_copy(src, dst, lsem.at[len(local) - len(tiles) + SLOTS if sem is None else sem])
         made.start()
         local.append(made)
         return len(local) - 1
@@ -226,15 +228,13 @@
             need_own(k, 1)
         for way in both if p else ():
             if p == 1 and piece == 0:
-                for kc in range(2):
-                    once(("oz", k, kc, way), held(p, way), lambda: g.at[0, k, unit(p, way), kc], along(-step(way)))
+                once(("oz", k, 0, way), held(p, way), lambda: g.at[0, k, unit(p, way)], along(-step(way)))
             else:
                 once(("gz", p - 1, k, way, piece), held(p, way), lambda: ref_z(p, k, way, piece), along(-step(way)))
 
     def need_y(p, k):
         if p == 0:
-            for kc in range(2):
-                once(("oy", k, kc), None, lambda: g.at[1, k, z, kc], beside)
+            once(("oy", k, 0), None, lambda: g.at[1, k, z], beside)
         for way in both if p else ():
             once(("gy", p, k, way), held(p, way), lambda: ref_y(p, k, way, 1), beside)
 
@@ -433,7 +433,7 @@
         at = slice(i * TILE, (i + 1) * TILE)
         gw[slot] = jnp.dot(gt[...], g[:, :, :, :, :, at].reshape(tokens, TILE), preferred_element_type=F32)
         lo = i * TILE % each
-        tiles.append(copy(gw.at[slot], gw_outs[i * TILE // each].at[:, lo:lo + TILE]))
+        tiles.append(copy(gw.at[slot], gw_outs[i * TILE // each].at[:, lo:lo + TILE], slot))
 
     def last_b(k):
         add_last("sb", k)
@@ -537,7 +537,7 @@
             pltpu.VMEM((SLOTS, width, TILE), F32),
             pltpu.SemaphoreType.DMA((1,)),
             pltpu.SemaphoreType.DMA((n_sems,)),
-            pltpu.SemaphoreType.DMA((6 + na + cols // TILE,)),
+            pltpu.SemaphoreType.DMA((6 + na + SLOTS,)),
         ],
         compiler_params=pltpu.CompilerParams(
             collective_id=0, has_side_effects=True, vmem_limit_bytes=VMEM_LIMIT

time: 77 us -> 76.9 us (level)
  no operation moved by 1% of the time
where the time goes in v7:
time: 76.9 us; the launch traced here: 76.7 us
  Pallas kernels  76.1 us (99%)
    pallas_call x1, Pallas kernels, fused(): pl.pallas_call(functools.partial(kernel, nh, nd), out_shape=(jax.ShapeDty...  72.4 us
    pallas_call x1, Pallas kernels, fused(): pl.pallas_call(hand_over, out_shape=(jax.ShapeDtypeStruct(grad_out.shape,...  3.67 us

profile of v7, /device:TPU:0, one launch (start us, length us, event | category | flops | bytes accessed | tf_op | source)
XLA Modules:
  0.0 76.7 jit_solution(16392790461547806861)
XLA Ops:
  0.6 72.4 %shard_map.76 = (bf16[4,32,2048]{2,1,0:T(8,128)(2,1)S(1)}, bf16[4,2,32,1024]{3,2,1,0:T(8,128)(2,1)S(1)}, f32[1024,512]{1,0:T(8,128)S(1)}, f32[1024,512]{1,0:T(8,...) custom-call(bf16[256,1024]{1,0:T(8,128)(2,1)} %attn.1, s32[8]{0:T(128)} %mask_hbm.1, f32[8]{0:T(128)} %scale_hbm.1, ...), custom_call_target="tpu_custom_call" | custom-call | tf_op jit(solution)/shard_map/pallas_call | solution.py:503
  73.1 3.7 %shard_map.77 = (bf16[32,8192]{1,0:T(8,128)(2,1)}, bf16[256,1024]{1,0:T(8,128)(2,1)}, f32[1024,2048]{1,0:T(8,128)}) custom-call(bf16[4,32,2048]{2,1,0:T(8,128)(2,1)S(1)} %get-tuple-element.9.pj, bf16[256,1024]{1,0:T(8,128)(2,1)S(1)} %bitcast.1, f32[1024,512]{1,0:T(8,128)S(1)} %get-tuple-element.11.refs_0_, f32[1024,512]{1,0:T(8,128)S(1)} %get-tuple-element.12.refs_1_, ...), custom_call_target="tpu_custom_call" | custom-call | tf_op jit(solution)/shard_map/pallas_call | solution.py:546
